TPU v7x, 256 devices: a whole 4x4x8 slice. The times are simulated.
256 devices in a mesh: lat: 8 (over x, z_hi), lon: 32 (over z_lo, y, core).
Axes of the slice: x: 4, y: 4, z: 8 (z_hi: 2, z_lo: 4; z = z_hi * 4 + z_lo), core: 2. Of those that a mesh axis runs over, the one named last changes fastest.
Arguments:
- fields: bfloat16 [64, 1024, 768], P('lat', 'lon'), may hold values from -60 to 60
- conv_kernel: float32 [3, 3, 768], replicated, may hold values from -1 to 1
- layer_norm_gain: float32 [768], replicated, may hold values from 0.1 to 1.9
- qkv_weight: bfloat16 [768, 2304], replicated, may hold values from -0.21875 to 0.21875
- out_weight: bfloat16 [768, 768], replicated, may hold values from -0.21875 to 0.21875
- score_bias: float32 [24, 64, 64], replicated, may hold values from -4 to 400
- pattern: int32 [8, 32, 256], P('lat', 'lon'), may hold values from 0 to 255, each once within a row
- cotangent: bfloat16 [64, 1024, 768], P('lat', 'lon'), may hold values from -6 to 6
Outputs:
- block_out: bfloat16 [64, 1024, 768], P('lat', 'lon')
- grad_fields: bfloat16 [64, 1024, 768], P('lat', 'lon')
- grad_project: float32 [768, 768], P('lat', 'lon')
- grad_kernel: float32 [3, 3, 768], replicated
- gain_gradient: float32 [768], replicated
Inputs may be any that keep to these rules, and one draw needn't show every extreme that they name: pattern[a, b, :] lists each of the 256 cells of block (a, b) once.
All inputs are finite; a program needn't handle non-finite values.
Results may differ from a plain program's by a relative error of at most 0.028.
Values may be sent and summed in bfloat16 or wider, within the bound.
A program may use at most 128 MiB of HBM per device.

v0:
```python
import math

import jax
import jax.numpy as jnp
from jax import lax
from jax.sharding import PartitionSpec as P

HEADS = 24
HEAD_DIM = 32
GROUP = 64


epsilon = 1e-05


def extended(array, sides, width, wrap):
    for axis, dim in sides:
        peers, length = (lax.axis_size(axis), array.shape[dim])
        up = [(i, (i + 1) % peers) for i in range(peers if wrap else peers - 1)]
        down = [(j, i) for i, j in up]
        last = lax.slice_in_dim(array, length - width, length, axis=dim)
        first = lax.slice_in_dim(array, 0, width, axis=dim)
        before = lax.ppermute(last, axis, up)
        after = lax.ppermute(first, axis, down)
        array = jnp.concatenate([before, array, after], axis=dim)
    return array


def widened(field):
    beside_all = extended(field, (("lon", 1),), 1, True)
    return extended(beside_all, (("lat", 0),), 1, False)


def apply_taps(padded, conv_kernel, lat_rows, lon_cols):
    summed = jnp.zeros((lat_rows, lon_cols, padded.shape[2]), jnp.float32)
    for lat_tap in range(3):
        for lon_tap in range(3):
            summed = (
                summed
                + conv_kernel[lat_tap, lon_tap]
                * padded[lat_tap : lat_tap + lat_rows, lon_tap : lon_tap + lon_cols]
            )
    return summed


def to_owner(packed):
    arrived = lax.all_to_all(
        lax.all_to_all(packed, "lat", split_axis=0, concat_axis=3, tiled=True),
        "lon",
        split_axis=1,
        concat_axis=4,
        tiled=True,
    )
    return arrived.reshape(-1, arrived.shape[-1])


def to_grid(packed):
    arrived = lax.all_to_all(
        lax.all_to_all(packed, "lat", split_axis=3, concat_axis=0, tiled=True),
        "lon",
        split_axis=4,
        concat_axis=1,
        tiled=True,
    )
    return arrived.reshape(-1, arrived.shape[-1])


def attention_probs(queries, key_rows, score_bias):
    scores = jnp.einsum("gihd,gjhd->ghij", queries, key_rows, preferred_element_type=jnp.float32)
    scores = scores * queries.shape[-1] ** (-0.5) + score_bias[None]
    peak = jnp.max(scores, axis=-1, keepdims=True)
    lifted = jnp.exp(scores - peak)
    return lifted / jnp.sum(lifted, axis=-1, keepdims=True)


def body(
    fields, conv_kernel, layer_norm_gain, qkv_weight, out_weight, score_bias, pattern, cotangent
):
    lat_rows, lon_cols, feature_count = fields.shape
    cell_count = lat_rows * lon_cols
    lat_count = lax.axis_size("lat")
    lon_count = lax.axis_size("lon")
    slot_count = cell_count // (lat_count * lon_count)
    scale_everywhere = 1.0 / math.sqrt(cell_count * lat_count * lon_count)
    head_scale = HEAD_DIM ** (-0.5)
    group_count = cell_count // GROUP
    slot_order = pattern.reshape(cell_count)
    inverse = (
        jnp.zeros((cell_count,), jnp.int32)
        .at[slot_order]
        .set(jnp.arange(cell_count, dtype=jnp.int32))
    )

    def outward(field):
        picked = jnp.take(field.reshape(cell_count, feature_count), slot_order, axis=0)
        return picked.reshape(lat_count, lon_count, slot_count, 1, 1, feature_count)

    def inward(grouped):
        return grouped.reshape(1, 1, slot_count, lat_count, lon_count, grouped.shape[-1])

    def homeward(flat):
        return jnp.take(flat, inverse, axis=0).reshape(lat_rows, lon_cols, feature_count)

    padded_fields = widened(fields)
    state_h = (
        fields.astype(jnp.float32) + apply_taps(padded_fields, conv_kernel, lat_rows, lon_cols)
    ).astype(jnp.bfloat16)
    state_f = state_h.astype(jnp.float32)
    mean_h = jnp.mean(state_f, axis=-1, keepdims=True)
    mean_removed = state_f - mean_h
    var_h = jnp.mean(mean_removed * mean_removed, axis=-1, keepdims=True)
    inverse_deviation = lax.rsqrt(var_h + epsilon)
    standardized_input = mean_removed * inverse_deviation
    normalized_fields = (standardized_input * layer_norm_gain).astype(jnp.bfloat16)
    normed_g = to_owner(outward(normalized_fields))
    cot_g = to_owner(outward(cotangent))
    qkv_rows = jnp.dot(normed_g, qkv_weight, preferred_element_type=jnp.float32).astype(
        jnp.bfloat16
    )
    split_rows = qkv_rows.reshape(group_count, GROUP, 3, HEADS, HEAD_DIM)
    queries = split_rows[:, :, 0]
    key_rows = split_rows[:, :, 1]
    value_rows = split_rows[:, :, 2]
    probs = attention_probs(queries, key_rows, score_bias)
    probs_low = probs.astype(jnp.bfloat16)
    attended = jnp.einsum(
        "ghij,gjhd->gihd", probs_low, value_rows, preferred_element_type=jnp.float32
    )
    attended = attended.astype(jnp.bfloat16).reshape(cell_count, feature_count)
    mixed = jnp.dot(attended, out_weight, preferred_element_type=jnp.float32).astype(jnp.bfloat16)
    mixed_flat = to_grid(inward(mixed))
    rows_summed = lax.psum_scatter(
        lax.dot_general(
            attended, cot_g, (((0,), (0,)), ((), ())), preferred_element_type=jnp.float32
        ).astype(jnp.bfloat16),
        "lat",
        scatter_dimension=0,
        tiled=True,
    )
    grad_project = (
        lax.psum_scatter(rows_summed, "lon", scatter_dimension=1, tiled=True).astype(jnp.float32)
        * scale_everywhere
    )
    grad_att = lax.dot_general(
        cot_g, out_weight, (((1,), (1,)), ((), ())), preferred_element_type=jnp.float32
    ).astype(jnp.bfloat16)
    grad_heads = grad_att.reshape(group_count, GROUP, HEADS, HEAD_DIM)
    held_query, held_key = (queries, key_rows)
    grad_probs = jnp.einsum(
        "gihd,gjhd->ghij", grad_heads, value_rows, preferred_element_type=jnp.float32
    )
    grad_scores = probs * (grad_probs - jnp.sum(probs * grad_probs, axis=-1, keepdims=True))
    grad_scores = grad_scores.astype(jnp.bfloat16)
    grad_query = (
        jnp.einsum("ghij,gjhd->gihd", grad_scores, held_key, preferred_element_type=jnp.float32)
        * head_scale
    )
    grad_key = (
        jnp.einsum("ghij,gihd->gjhd", grad_scores, held_query, preferred_element_type=jnp.float32)
        * head_scale
    )
    grad_value = jnp.einsum(
        "ghij,gihd->gjhd", probs_low, grad_heads, preferred_element_type=jnp.float32
    )
    grad_qkv = jnp.stack([grad_query, grad_key, grad_value], axis=2).astype(jnp.bfloat16)
    grad_qkv = grad_qkv.reshape(cell_count, 3 * feature_count)
    grad_grouped = lax.dot_general(
        grad_qkv, qkv_weight, (((1,), (1,)), ((), ())), preferred_element_type=jnp.float32
    ).astype(jnp.bfloat16)
    grad_flat = to_grid(inward(grad_grouped))
    block_out = (state_f + homeward(mixed_flat).astype(jnp.float32)).astype(jnp.bfloat16)
    normalized_gradient = homeward(grad_flat).astype(jnp.float32)
    gain_on_device = jnp.sum(normalized_gradient * standardized_input, axis=(0, 1))
    gain_scaled = normalized_gradient * layer_norm_gain
    layer_norm_gradient = inverse_deviation * (
        gain_scaled
        - jnp.mean(gain_scaled, axis=-1, keepdims=True)
        - standardized_input * jnp.mean(gain_scaled * standardized_input, axis=-1, keepdims=True)
    )
    grad_h = (cotangent.astype(jnp.float32) + layer_norm_gradient).astype(jnp.bfloat16)
    grad_hf = grad_h.astype(jnp.float32)
    padded_grad = widened(grad_h)
    grad_fields = (
        grad_hf + apply_taps(padded_grad, conv_kernel[::-1, ::-1], lat_rows, lon_cols)
    ).astype(jnp.bfloat16)
    kernel_terms = []
    for lat_tap in range(3):
        for lon_tap in range(3):
            kernel_terms.append(
                jnp.sum(
                    padded_fields[lat_tap : lat_tap + lat_rows, lon_tap : lon_tap + lon_cols]
                    * grad_hf,
                    axis=(0, 1),
                )
            )
    kernel_local = jnp.stack(kernel_terms).reshape(3, 3, feature_count)
    gain_total, kernel_total = lax.psum((gain_on_device, kernel_local), ("lat", "lon"))
    return (
        block_out,
        grad_fields,
        grad_project,
        kernel_total * scale_everywhere,
        gain_total * scale_everywhere,
    )


def solution(mesh):
    placed = (
        P("lat", "lon", None),
        P(),
        P(),
        P(),
        P(),
        P(),
        P("lat", "lon", None),
        P("lat", "lon", None),
    )
    return jax.shard_map(
        body,
        mesh=mesh,
        in_specs=placed,
        out_specs=(P("lat", "lon", None), P("lat", "lon", None), P("lat", "lon"), P(), P()),
        check_vma=False,
    )
```

profile of v0, /device:TPU:1, one launch (start us, length us, event | category | flops | bytes accessed | tf_op | source)
XLA Modules:
  0.0 629.2 jit_solution(4152701214273472165)
XLA Ops:
  8.3 2.8 collective-permute-start
  17.3 8.8 %collective-permute-start.2 = (bf16[1,34,768]{2,1,0:T(8,128)(2,1)}, bf16[1,34,768]{2,1,0:T(8,128)(2,1)}, u32[]{:S(2)}, u32[]{:S(2)}) collective-permute-start(bf16[1,34,768]{2,1,0:T(8,128)(2,1)} %get-tuple-element.66), channel_id=1, source_target_pairs={{0,32},{32,64},{64,96},{96,128},{128,160},{160,192},{192,224},{1,3... | collective-permute-start | bytes 156680 | tf_op jit(solution)/shard_map/ppermute | solution.py:23
  27.4 3.2 gather_fusion.2
  30.7 4.7 collective-permute-done.3
  40.1 3.3 gather_fusion
  45.4 15.7 %all_to_all.108 = bf16[8,32,1,1,1,768]{5,1,4,3,2,0:T(8,128)(2,1)} all-to-all(bf16[8,32,1,1,1,768]{5,1,4,3,2,0:T(8,128)(2,1)S(1)} %bitcast.110), channel_id=1, replica_groups=mesh['lat'=8,'lon'=32] {'lat'}, dimensions={0} | all-to-all | bytes 786432 | tf_op jit(solution)/shard_map/all_to_all | solution.py:48
  61.1 4.1 all-to-all-start
  67.2 8.8 %all-to-all-done = bf16[8,32,1,1,1,768]{5,1,4,3,2,0:T(8,128)(2,1)} async-done(((bf16[8,32,1,1,1,768]{5,1,4,3,2,0:T(8,128)(2,1)}), bf16[8,32,1,1,1,768]{5,1,4,3,2,0:T(8,128)(2,1)}, u32[]{:S(2)}, u32[]{:S(2)}) %all-to-all-start) | async-done | bytes 393248 | tf_op jit(solution)/shard_map/all_to_all | solution.py:48
  75.9 17.9 %all-to-all-start.5 = ((bf16[1,32,1,8,1,768]{5,3,4,2,0,1:T(8,128)(2,1)}), bf16[1,32,1,8,1,768]{5,3,4,2,0,1:T(8,128)(2,1)}, u32[]{:S(2)}, u32[]{:S(2)}) async-start(bf16[1,32,1,8,1,768]{5,3,4,2,0,1:T(8,128)(2,1)} %copy.78), calls=%async_computation.5 | async-start | bytes 786432 | tf_op jit(solution)/shard_map/all_to_all | solution.py:47
  95.8 11.9 %all-to-all-done.5 = bf16[1,32,1,8,1,768]{5,3,4,2,0,1:T(8,128)(2,1)} async-done(((bf16[1,32,1,8,1,768]{5,3,4,2,0,1:T(8,128)(2,1)}), bf16[1,32,1,8,1,768]{5,3,4,2,0,1:T(8,128)(2,1)}, u32[]{:S(2)}, u32[]{:S(2)}) %all-to-all-start.5) | async-done | bytes 393248 | tf_op jit(solution)/shard_map/all_to_all | solution.py:47
  107.6 4.8 all-to-all-start.1
  131.8 4.6 reshape.150
  145.4 3.2 multiply_reduce_fusion
  155.4 4.3 all-to-all-start.2
  159.6 3.9 multiply_convert_fusion
  166.4 4.5 copy.86
  170.8 4.5 convert_element_type.159
  175.3 3.1 convolution_convert_fusion.4
  178.5 9.0 %all-to-all-start.6 = ((bf16[1,1,1,8,32,768]{5,4,2,1,0,3:T(8,128)(2,1)}), bf16[1,1,1,8,32,768]{5,4,2,1,0,3:T(8,128)(2,1)}, u32[]{:S(2)}, u32[]{:S(2)}) async-start(bf16[1,1,1,8,32,768]{5,4,2,1,0,3:T(8,128)(2,1)} %bitcast.112), calls=%async_computation.6 | async-start | bytes 786432 | tf_op jit(solution)/shard_map/all_to_all | solution.py:59
  189.5 10.5 %all-to-all-done.6 = bf16[1,1,1,8,32,768]{5,4,2,1,0,3:T(8,128)(2,1)} async-done(((bf16[1,1,1,8,32,768]{5,4,2,1,0,3:T(8,128)(2,1)}), bf16[1,1,1,8,32,768]{5,4,2,1,0,3:T(8,128)(2,1)}, u32[]{:S(2)}, u32[]{:S(2)}) %all-to-all-start.6) | async-done | bytes 393248 | tf_op jit(solution)/shard_map/all_to_all | solution.py:59
  199.9 9.4 %all-to-all-start.3 = ((bf16[8,1,1,1,32,768]{5,0,3,2,1,4:T(8,128)(2,1)}), bf16[8,1,1,1,32,768]{5,0,3,2,1,4:T(8,128)(2,1)}, u32[]{:S(2)}, u32[]{:S(2)}) async-start(bf16[8,1,1,1,32,768]{5,0,3,2,1,4:T(8,128)(2,1)} %copy.75), calls=%async_computation.3 | async-start | bytes 786432 | tf_op jit(solution)/shard_map/all_to_all | solution.py:58
  217.1 6.0 all-to-all-done.3
  223.1 4.4 all-to-all-start.7
  234.8 3.4 gather_fusion.1
  238.2 3.0 all-to-all-done.7
  243.0 3.3 gather_fusion.3
  252.8 3.2 fusion.45
  267.4 77.1 %all-reduce.1 = (f32[3,3,768]{2,1,0:T(4,128)}, f32[768]{0:T(1024)}) all-reduce(f32[3,3,768]{2,1,0:T(4,128)} %reshape.161, f32[768]{0:T(1024)} %get-tuple-element.35), channel_id=1, replica_groups=mesh['lat'=8,'lon'=32] {'lat','lon'}, use_global_device_ids=true, to_apply=%region_19.21 | all-reduce | flops 7680 | bytes 61440 | tf_op jit(solution)/shard_map/psum | solution.py:197
  346.8 3.8 collective-permute-start.6
  353.1 6.3 collective-permute-done.7
  362.1 4.3 fusion.36
  366.4 252.8 %all-reduce.4.cloned.1.call-done = bf16[96,768]{1,0:T(8,128)(2,1)} async-done(((bf16[96,768]{1,0:T(8,128)(2,1)}), bf16[96,768]{1,0:T(8,128)(2,1)}) %all-reduce.4.cloned.1.call-update) | async-done | bytes 147472
  (172 shorter events, 103.5 us)
Async XLA Ops:
  7.2 120.1 %copy-start = (bf16[768,2304]{1,0:T(8,128)(2,1)S(1)}, bf16[768,2304]{1,0:T(8,128)(2,1)}, u32[]{:S(2)}) copy-start(bf16[768,2304]{1,0:T(8,128)(2,1)} %param.13) | copy-start | bytes 10616836
  8.3 6.9 %collective-permute-start = (bf16[8,1,768]{2,1,0:T(2,128)(2,1)S(1)}, bf16[8,1,768]{2,1,0:T(2,128)(2,1)S(1)}, u32[]{:S(2)}, u32[]{:S(2)}) collective-permute-start(bf16[8,1,768]{2,1,0:T(2,128)(2,1)S(1)} %get-tuple-element.71), channel_id=1, source_target_pairs={{0,1},{1,2},{2,3},{3,4},{4,5},{5,6},{6,7},{7,8},{8,9},{9,10},{10,1... | collective-permute-start | bytes 36872 | tf_op jit(solution)/shard_map/ppermute | solution.py:23
  11.1 4.1 collective-permute-start.1
  15.2 23.2 %copy-start.28 = (f32[768]{0:T(1024)}, f32[768]{0:T(1024)S(1)}, u32[]{:S(2)}) copy-start(f32[768]{0:T(1024)S(1)} %get-tuple-element.44) | copy-start | bytes 9220
  15.2 23.2 %copy-start.30 = (f32[768]{0:T(1024)}, f32[768]{0:T(1024)S(1)}, u32[]{:S(2)}) copy-start(f32[768]{0:T(1024)S(1)} %get-tuple-element.45) | copy-start | bytes 9220
  17.3 13.4 %collective-permute-start.2 = (bf16[1,34,768]{2,1,0:T(8,128)(2,1)}, bf16[1,34,768]{2,1,0:T(8,128)(2,1)}, u32[]{:S(2)}, u32[]{:S(2)}) collective-permute-start(bf16[1,34,768]{2,1,0:T(8,128)(2,1)} %get-tuple-element.66), channel_id=1, source_target_pairs={{0,32},{32,64},{64,96},{96,128},{128,160},{160,192},{192,224},{1,3... | collective-permute-start | bytes 156680 | tf_op jit(solution)/shard_map/ppermute | solution.py:23
  26.1 9.3 %collective-permute-start.3 = (bf16[1,34,768]{2,1,0:T(8,128)(2,1)}, bf16[1,34,768]{2,1,0:T(8,128)(2,1)}, u32[]{:S(2)}, u32[]{:S(2)}) collective-permute-start(bf16[1,34,768]{2,1,0:T(8,128)(2,1)} %get-tuple-element.67), channel_id=1, source_target_pairs={{32,0},{64,32},{96,64},{128,96},{160,128},{192,160},{224,192},{33,... | collective-permute-start | bytes 156680 | tf_op jit(solution)/shard_map/ppermute | solution.py:24
  30.6 6.5 %copy-start.14 = (bf16[8,32,768]{2,1,0:T(8,128)(2,1)S(1)}, bf16[8,32,768]{2,1,0:T(8,128)(2,1)}, u32[]{:S(2)}) copy-start(bf16[8,32,768]{2,1,0:T(8,128)(2,1)} %param.10) | copy-start | bytes 1179652
  30.6 6.5 %copy-start.21 = (bf16[8,1,768]{2,1,0:T(2,128)(2,1)S(1)}, bf16[8,1,768]{2,1,0:T(2,128)(2,1)}, u32[]{:S(2)}) copy-start(bf16[8,1,768]{2,1,0:T(2,128)(2,1)} %copy-done.20) | copy-start | bytes 36868
  30.6 6.5 %copy-start.24 = (bf16[8,1,768]{2,1,0:T(2,128)(2,1)S(1)}, bf16[8,1,768]{2,1,0:T(2,128)(2,1)}, u32[]{:S(2)}) copy-start(bf16[8,1,768]{2,1,0:T(2,128)(2,1)} %copy-done.23) | copy-start | bytes 36868
  30.6 6.5 %copy-start.32 = (f32[768]{0:T(1024)S(1)}, f32[768]{0:T(1024)}, u32[]{:S(2)}) copy-start(f32[768]{0:T(1024)} %get-tuple-element.46) | copy-start | bytes 9220
  30.6 6.5 %copy-start.34 = (f32[768]{0:T(1024)S(1)}, f32[768]{0:T(1024)}, u32[]{:S(2)}) copy-start(f32[768]{0:T(1024)} %get-tuple-element.47) | copy-start | bytes 9220
  30.6 6.5 %copy-start.35 = (f32[768]{0:T(1024)S(1)}, f32[768]{0:T(1024)}, u32[]{:S(2)}) copy-start(f32[768]{0:T(1024)} %get-tuple-element.48) | copy-start | bytes 9220
  30.6 6.5 %copy-start.36 = (f32[768]{0:T(1024)S(1)}, f32[768]{0:T(1024)}, u32[]{:S(2)}) copy-start(f32[768]{0:T(1024)} %get-tuple-element.49) | copy-start | bytes 9220
  30.6 6.5 %copy-start.37 = (f32[768]{0:T(1024)S(1)}, f32[768]{0:T(1024)}, u32[]{:S(2)}) copy-start(f32[768]{0:T(1024)} %get-tuple-element.50) | copy-start | bytes 9220
  30.7 6.5 %copy-start.38 = (f32[768]{0:T(1024)S(1)}, f32[768]{0:T(1024)}, u32[]{:S(2)}) copy-start(f32[768]{0:T(1024)} %get-tuple-element.51) | copy-start | bytes 9220
  61.1 14.9 %all-to-all-start = ((bf16[8,32,1,1,1,768]{5,1,4,3,2,0:T(8,128)(2,1)}), bf16[8,32,1,1,1,768]{5,1,4,3,2,0:T(8,128)(2,1)}, u32[]{:S(2)}, u32[]{:S(2)}) async-start(bf16[8,32,1,1,1,768]{5,1,4,3,2,0:T(8,128)(2,1)} %bitcast.109), calls=%async_computation | async-start | bytes 786432 | tf_op jit(solution)/shard_map/all_to_all | solution.py:48
  75.9 31.7 %all-to-all-start.5 = ((bf16[1,32,1,8,1,768]{5,3,4,2,0,1:T(8,128)(2,1)}), bf16[1,32,1,8,1,768]{5,3,4,2,0,1:T(8,128)(2,1)}, u32[]{:S(2)}, u32[]{:S(2)}) async-start(bf16[1,32,1,8,1,768]{5,3,4,2,0,1:T(8,128)(2,1)} %copy.78), calls=%async_computation.5 | async-start | bytes 786432 | tf_op jit(solution)/shard_map/all_to_all | solution.py:47
  107.6 18.6 %all-to-all-start.1 = ((bf16[1,32,1,8,1,768]{5,3,4,2,0,1:T(8,128)(2,1)}), bf16[1,32,1,8,1,768]{5,3,4,2,0,1:T(8,128)(2,1)}, u32[]{:S(2)}, u32[]{:S(2)}) async-start(bf16[1,32,1,8,1,768]{5,3,4,2,0,1:T(8,128)(2,1)} %copy.65), calls=%async_computation.1 | async-start | bytes 786432 | tf_op jit(solution)/shard_map/all_to_all | solution.py:47
  155.4 23.1 %all-to-all-start.2 = ((bf16[1,1,1,8,32,768]{5,4,2,1,0,3:T(8,128)(2,1)}), bf16[1,1,1,8,32,768]{5,4,2,1,0,3:T(8,128)(2,1)}, u32[]{:S(2)}, u32[]{:S(2)}) async-start(bf16[1,1,1,8,32,768]{5,4,2,1,0,3:T(8,128)(2,1)} %bitcast.111), calls=%async_computation.2 | async-start | bytes 786432 | tf_op jit(solution)/shard_map/all_to_all | solution.py:59
  178.5 21.4 %all-to-all-start.6 = ((bf16[1,1,1,8,32,768]{5,4,2,1,0,3:T(8,128)(2,1)}), bf16[1,1,1,8,32,768]{5,4,2,1,0,3:T(8,128)(2,1)}, u32[]{:S(2)}, u32[]{:S(2)}) async-start(bf16[1,1,1,8,32,768]{5,4,2,1,0,3:T(8,128)(2,1)} %bitcast.112), calls=%async_computation.6 | async-start | bytes 786432 | tf_op jit(solution)/shard_map/all_to_all | solution.py:59
  199.9 23.2 %all-to-all-start.3 = ((bf16[8,1,1,1,32,768]{5,0,3,2,1,4:T(8,128)(2,1)}), bf16[8,1,1,1,32,768]{5,0,3,2,1,4:T(8,128)(2,1)}, u32[]{:S(2)}, u32[]{:S(2)}) async-start(bf16[8,1,1,1,32,768]{5,0,3,2,1,4:T(8,128)(2,1)} %copy.75), calls=%async_computation.3 | async-start | bytes 786432 | tf_op jit(solution)/shard_map/all_to_all | solution.py:58
  223.1 18.1 %all-to-all-start.7 = ((bf16[8,1,1,1,32,768]{5,0,3,2,1,4:T(8,128)(2,1)}), bf16[8,1,1,1,32,768]{5,0,3,2,1,4:T(8,128)(2,1)}, u32[]{:S(2)}, u32[]{:S(2)}) async-start(bf16[8,1,1,1,32,768]{5,0,3,2,1,4:T(8,128)(2,1)} %copy.88), calls=%async_computation.7 | async-start | bytes 786432 | tf_op jit(solution)/shard_map/all_to_all | solution.py:58
  227.5 134.6 %reduce-scatter.3.cloned.1.call-start = ((), (), s32[]{:S(2)}) async-start(), calls=%async_computation.9 | async-start | bytes 1327104 | tf_op jit(solution)/shard_map/reduce_scatter | solution.py:132
  230.2 389.0 %all-reduce.4.cloned.1.call-start = ((), (), s32[]{:S(2)}) async-start(), calls=%async_computation.10 | async-start | bytes 294912
  255.9 106.2 %copy-start.29 = (f32[768]{0:T(1024)S(1)}, f32[768]{0:T(1024)}, u32[]{:S(2)}) copy-start(f32[768]{0:T(1024)} %copy-done.28) | copy-start | bytes 9220
  255.9 106.2 %copy-start.31 = (f32[768]{0:T(1024)S(1)}, f32[768]{0:T(1024)}, u32[]{:S(2)}) copy-start(f32[768]{0:T(1024)} %copy-done.30) | copy-start | bytes 9220
  255.9 106.2 %copy-start.33 = (f32[768]{0:T(1024)S(1)}, f32[768]{0:T(1024)}, u32[]{:S(2)}) copy-start(f32[768]{0:T(1024)} %get-tuple-element.46) | copy-start | bytes 9220
  266.9 79.0 %collective-permute-start.4 = (bf16[8,1,768]{2,1,0:T(2,128)(2,1)}, bf16[8,1,768]{2,1,0:T(2,128)(2,1)}, u32[]{:S(2)}, u32[]{:S(2)}) collective-permute-start(bf16[8,1,768]{2,1,0:T(2,128)(2,1)} %get-tuple-element.68), channel_id=1, source_target_pairs={{0,1},{1,2},{2,3},{3,4},{4,5},{5,6},{6,7},{7,8},{8,9},{9,10},{10,1... | collective-permute-start | bytes 36872 | tf_op jit(solution)/shard_map/ppermute | solution.py:23
  266.9 79.0 %collective-permute-start.5 = (bf16[8,1,768]{2,1,0:T(2,128)(2,1)}, bf16[8,1,768]{2,1,0:T(2,128)(2,1)}, u32[]{:S(2)}, u32[]{:S(2)}) collective-permute-start(bf16[8,1,768]{2,1,0:T(2,128)(2,1)} %get-tuple-element.69), channel_id=1, source_target_pairs={{1,0},{2,1},{3,2},{4,3},{5,4},{6,5},{7,6},{8,7},{9,8},{10,9},{11,1... | collective-permute-start | bytes 36872 | tf_op jit(solution)/shard_map/ppermute | solution.py:24
  346.8 6.4 %collective-permute-start.6 = (bf16[1,34,768]{2,1,0:T(8,128)(2,1)S(1)}, bf16[1,34,768]{2,1,0:T(8,128)(2,1)S(1)}, u32[]{:S(2)}, u32[]{:S(2)}) collective-permute-start(bf16[1,34,768]{2,1,0:T(8,128)(2,1)S(1)} %get-tuple-element.62), channel_id=1, source_target_pairs={{0,32},{32,64},{64,96},{96,128},{128,160},{160,192},{192,224},{1,3... | collective-permute-start | bytes 156680 | tf_op jit(solution)/shard_map/ppermute | solution.py:23
  350.5 8.9 %collective-permute-start.7 = (bf16[1,34,768]{2,1,0:T(8,128)(2,1)S(1)}, bf16[1,34,768]{2,1,0:T(8,128)(2,1)S(1)}, u32[]{:S(2)}, u32[]{:S(2)}) collective-permute-start(bf16[1,34,768]{2,1,0:T(8,128)(2,1)S(1)} %get-tuple-element.63), channel_id=1, source_target_pairs={{32,0},{64,32},{96,64},{128,96},{160,128},{192,160},{224,192},{33,... | collective-permute-start | bytes 156680 | tf_op jit(solution)/shard_map/ppermute | solution.py:24
  (27 other events, 44.7 us)
Sparse Core Ops, SparseCore 0:
  232.3 83.6 reduce-scatter.2
  362.2 256.9 all-reduce.3
where the time goes:
time: 638 us; the launch traced here: 629 us
  waiting for transfers between devices  307 us (48%)
  blocking collectives  92.7 us (15%)
  local copies, waits for them, and re-layouts  80.9 us (13%)
  starting transfers between devices  73.1 us (11%)
  other arithmetic  39.4 us (6%)
  matrix products  20.8 us (3%)
  between operations  15.6 us (2%)
    unnamed x3, waiting for transfers between devices  253 us
    psum x1, blocking collectives, body(): lax.psum((gain_on_device, kernel_local), ('lat', 'lon'))  77.1 us
    all_to_all x2, starting transfers between devices, to_owner(): lax.all_to_all(lax.all_to_all(packed, 'lat', split_axis=0, concat_axis=3,...  22.7 us
    all_to_all x1, blocking collectives, to_owner(): lax.all_to_all(packed, 'lat', split_axis=0, concat_axis=3, tiled=True)  15.7 us
    ppermute x4, starting transfers between devices, extended(): before = lax.ppermute(last, axis, up)  15.3 us
    all_to_all x2, waiting for transfers between devices, to_owner(): lax.all_to_all(lax.all_to_all(packed, 'lat', split_axis=0, concat_axis=3,...  14.5 us
    all_to_all x2, starting transfers between devices, to_grid(): lax.all_to_all(lax.all_to_all(packed, 'lat', split_axis=3, concat_axis=0,...  13.7 us
    all_to_all x2, starting transfers between devices, to_grid(): lax.all_to_all(packed, 'lat', split_axis=3, concat_axis=0, tiled=True)  13.3 us
  transfers between devices with their start and end apart: 17, of which 9 were waited for; matrix products, arithmetic and copies ran while one was open for 15% of the time, Pallas kernels for 0%

commit v1 on v0

v1 whole, which is shorter than its diff:
```python
import math

import jax
import jax.numpy as jnp
from jax import lax
from jax.experimental import pallas as pl
from jax.experimental.pallas import tpu as pltpu
from jax.sharding import PartitionSpec as P

MESH = pl.DeviceIdType.MESH
BF = jnp.bfloat16
F32 = jnp.float32
D = 768
EPS = 1e-05
HEAD_SCALE = 32 ** (-0.5)
TOTAL_SCALE = 1.0 / math.sqrt(65536)


def nn(a, b):
    return lax.dot_general(a, b, (((1,), (0,)), ((), ())), preferred_element_type=F32)


def nt(a, b):
    return lax.dot_general(a, b, (((1,), (1,)), ((), ())), preferred_element_type=F32)


def tn(a, b):
    return lax.dot_general(a, b, (((0,), (0,)), ((), ())), preferred_element_type=F32)


def device(x, y, z, c):
    return (x * 2 + z // 4, (z % 4) * 8 + y * 2 + c)


def one_hot(cond):
    return jnp.where(cond, 1.0, 0.0).astype(BF)


def iota2(axis):
    return lax.broadcasted_iota(jnp.int32, (256, 256), axis)


def slot_order(s):
    x, zh, zl, y, c = s >> 6, (s >> 5) & 1, (s >> 3) & 3, (s >> 1) & 3, s & 1
    return x * 64 + y * 16 + zh * 8 + zl * 2 + c


def arrival_order(p):
    x, zh, zl, y, c = p >> 6, (p >> 5) & 1, (p >> 3) & 3, (p >> 1) & 3, p & 1
    return zh * 128 + zl * 32 + c * 16 + x * 4 + y


def kernel(
    fields, cot, taps, gain, pat, wqkv_hbm, wo_hbm, bias_hbm,
    block_out, grad_fields, gp_out, sums_out,
    wqkv, wo, bias, bias_t, w_sem,
    edges, edges_g, rows_in, cols_in, rows_in_g, cols_in_g, halo_s, halo_r, halo_gs, halo_gr,
    shifted, hid, xhat, rstd, work, work2, normed_w,
    perm_out, perm_home, perm_swap, perm_pos, perm_arr,
    c0, c1, c2, c3, n0, n1, n2, n3, g0, g1, g2, g3, m0, m1, m2, m3, a2a_s, a2a_r,
    cot_g, nrm_g, qkv, grad_att, att, gqkv,
    gp0, gp1, gp2, gp3, gp4, gp5, gp6, gp7, gpy_s, gpy_r, gpz_s, gpz_r, gpc_s, gpc_r, gpl_s, gpl_r,
    acc, s0, s1, s2, s3, s4, sum_s, sum_r,
):
    a = lax.axis_index("lat")
    b = lax.axis_index("lon")
    x, zh = a // 2, a % 2
    zl, y, c = b // 8, (b // 2) % 4, b % 2
    z = zh * 4 + zl
    me_b = x * 4 + y
    me_a = z * 2 + c

    def peer_b(k):
        return device(k // 4, k % 4, z, c)

    def peer_a(k):
        return device(x, y, k // 2, k % 2)

    def neighbour(da, db):
        return ((a + da + 8) % 8, (b + db + 32) % 32)

    loads = [
        pltpu.make_async_copy(wqkv_hbm, wqkv, w_sem.at[0]),
        pltpu.make_async_copy(wo_hbm, wo, w_sem.at[1]),
        pltpu.make_async_copy(bias_hbm, bias, w_sem.at[2]),
    ]
    for load in loads:
        load.start()

    bar = pltpu.get_barrier_semaphore()

    def greet(d, carry):
        pl.semaphore_signal(bar, inc=1, device_id=peer_b((me_b + d) % 16), device_id_type=MESH)
        pl.semaphore_signal(bar, inc=1, device_id=peer_a((me_a + d) % 16), device_id_type=MESH)
        return carry

    offsets = [(-1, 0), (1, 0), (0, -1), (0, 1), (-1, -1), (-1, 1), (1, -1), (1, 1)]
    for da, db in offsets:
        pl.semaphore_signal(bar, inc=1, device_id=neighbour(da, db), device_id_type=MESH)
    for d in range(1, 4):
        pl.semaphore_signal(
            bar, inc=1, device_id=device((x + d) % 4, y, (z + 4) % 8, c), device_id_type=MESH
        )
    lax.fori_loop(1, 16, greet, 0)

    row8 = lax.broadcasted_iota(jnp.int32, (8, D), 0)
    row32 = lax.broadcasted_iota(jnp.int32, (32, D), 0)

    def fill_edges(source, dest):
        left = jnp.zeros((8, D), F32)
        right = jnp.zeros((8, D), F32)
        for l in range(8):
            row = source[l].astype(F32)
            left = jnp.where(row8 == l, row[0:1, :], left)
            right = jnp.where(row8 == l, row[31:32, :], right)
        dest[0] = left.astype(BF)
        dest[1] = right.astype(BF)

    def halo_copies(source, edge, rows, cols, ss, rs):
        out = []
        routes = [
            (source.at[0], rows.at[1]), (source.at[7], rows.at[0]),
            (edge.at[0], cols.at[1]), (edge.at[1], cols.at[0]),
            (edge.at[0], cols.at[5]), (edge.at[1], cols.at[4]),
            (edge.at[0], cols.at[3]), (edge.at[1], cols.at[2]),
        ]
        for m, (src, dst) in enumerate(routes):
            out.append(
                pltpu.make_async_remote_copy(
                    src_ref=src, dst_ref=dst, send_sem=ss.at[m], recv_sem=rs.at[m],
                    device_id=neighbour(*offsets[m]), device_id_type=MESH,
                )
            )
        return out

    top_mask = (a > 0).astype(F32)
    bottom_mask = (a < 7).astype(F32)

    def fill_shifted(source, rows, cols):
        for r in range(10):
            if r == 0:
                f = rows[0].astype(F32) * top_mask
                le = cols[2].astype(F32)[7:8, :] * top_mask
                ri = cols[3].astype(F32)[7:8, :] * top_mask
            elif r == 9:
                f = rows[1].astype(F32) * bottom_mask
                le = cols[4].astype(F32)[0:1, :] * bottom_mask
                ri = cols[5].astype(F32)[0:1, :] * bottom_mask
            else:
                f = source[r - 1].astype(F32)
                le = cols[0].astype(F32)[r - 1 : r, :]
                ri = cols[1].astype(F32)[r - 1 : r, :]
            shifted[0, r] = jnp.where(row32 == 0, le, pltpu.roll(f, 1, 0))
            shifted[1, r] = f
            shifted[2, r] = jnp.where(row32 == 31, ri, pltpu.roll(f, 31, 0))

    def exchange(peer, me, src, dst, slot, sends):
        def step(d, carry):
            k = (me + d) % 16
            copy = pltpu.make_async_remote_copy(
                src_ref=src.at[k], dst_ref=dst.at[me] if sends else dst.at[k],
                send_sem=a2a_s.at[slot, d], recv_sem=a2a_r.at[slot, me if sends else k],
                device_id=peer(k), device_id_type=MESH,
            )
            if sends:
                copy.start()
            else:
                copy.wait()
            return carry

        lax.fori_loop(1, 16, step, 0)
        if sends:
            dst[me] = src[me]

    def permute(perm, src, dst):
        for n in range(3):
            cols = slice(n * 256, (n + 1) * 256)
            rows = src[..., cols].reshape(256, 256)
            got = nn(perm[...], rows).astype(BF)
            dst[..., cols] = got.reshape(dst.shape[:-1] + (256,))

    pat_hot = one_hot(iota2(0) == pat[...])
    order_hot = one_hot(iota2(0) == slot_order(iota2(1)))
    perm_out[...] = nt(order_hot, pat_hot).astype(BF)
    perm_home[...] = nt(pat_hot, order_hot).astype(BF)
    perm_swap[...] = one_hot(iota2(1) == (iota2(0) & 15) * 16 + (iota2(0) >> 4))
    perm_pos[...] = one_hot(iota2(1) == arrival_order(iota2(0)))
    perm_arr[...] = one_hot(iota2(0) == arrival_order(iota2(1)))
    fill_edges(fields, edges)
    permute(perm_out, cot, c0)

    pl.semaphore_wait(bar, 41)

    halos = halo_copies(fields, edges, rows_in, cols_in, halo_s, halo_r)
    for copy in halos:
        copy.start()
    exchange(peer_b, me_b, c0, c1, 0, True)

    loads[2].wait()
    for q in range(6):
        bias_t[q] = jnp.transpose(bias[4 * q : 4 * q + 4].reshape(256, 64))

    for copy in halos:
        copy.wait()
    fill_shifted(fields, rows_in, cols_in)
    gain_row = gain[...]

    def conv_row(l, flip):
        out = shifted[1, l + 1]
        for i in range(3):
            for j in range(3):
                t = 8 - (3 * i + j) if flip else 3 * i + j
                out = out + taps[t : t + 1, :] * shifted[j, l + i]
        return out

    def norm_row(l, carry):
        h = conv_row(l, False).astype(BF)
        hid[l] = h
        hf = h.astype(F32)
        mean = jnp.mean(hf, axis=-1, keepdims=True)
        rem = hf - mean
        var = jnp.mean(rem * rem, axis=-1, keepdims=True)
        inv = lax.rsqrt(var + EPS)
        xh = rem * inv
        xhat[l] = xh
        rstd[l] = inv
        normed_w[l] = (xh * gain_row).astype(BF)
        return carry

    lax.fori_loop(0, 8, norm_row, 0)
    permute(perm_out, normed_w, n0)
    exchange(peer_b, me_b, n0, n1, 1, True)

    exchange(peer_b, me_b, c0, c1, 0, False)
    permute(perm_swap, c1, c2)
    exchange(peer_a, me_a, c2, c3, 2, True)
    exchange(peer_b, me_b, n0, n1, 1, False)
    permute(perm_swap, n1, n2)
    exchange(peer_a, me_a, n2, n3, 3, True)

    exchange(peer_a, me_a, c2, c3, 2, False)
    permute(perm_pos, c3, cot_g)
    loads[1].wait()
    for n in range(3):
        cols = slice(n * 256, (n + 1) * 256)
        grad_att[:, cols] = nt(cot_g[...], wo[cols, :]).astype(BF)
    exchange(peer_a, me_a, n2, n3, 3, False)
    permute(perm_pos, n3, nrm_g)
    loads[0].wait()

    def project(n, carry):
        cols = pl.ds(pl.multiple_of(n * 256, 256), 256)
        qkv[:, cols] = nn(nrm_g[...], wqkv[:, cols]).astype(BF)
        return carry

    lax.fori_loop(0, 9, project, 0)

    lane_head = lax.broadcasted_iota(jnp.int32, (64, 128), 1) >> 5

    def spread(v):
        vf = v.astype(F32)
        return jnp.concatenate(
            [jnp.where(lane_head == e, vf, 0.0).astype(BF) for e in range(4)], axis=0
        )

    def gather(v):
        out = jnp.zeros((64, 128), F32)
        for e in range(4):
            out = jnp.where(lane_head == e, v[e * 64 : (e + 1) * 64, :], out)
        return out

    def attend(u, carry):
        q = u % 6
        rows = pl.ds(pl.multiple_of((u // 6) * 64, 64), 64)
        at = pl.multiple_of(q * 128, 128)
        qc = qkv[rows, pl.ds(at, 128)]
        kc = qkv[rows, pl.ds(pl.multiple_of(at + 768, 128), 128)]
        vc = qkv[rows, pl.ds(pl.multiple_of(at + 1536, 128), 128)]
        gc = grad_att[rows, pl.ds(at, 128)]
        q_bd = spread(qc)
        g_bd = spread(gc)
        st = nt(kc, q_bd) * HEAD_SCALE + bias_t[q]
        e = jnp.exp(st - jnp.max(st, axis=0, keepdims=True))
        p = e * (1.0 / jnp.sum(e, axis=0, keepdims=True))
        pb = p.astype(BF)
        att[rows, pl.ds(at, 128)] = gather(tn(pb, vc)).astype(BF)
        dp = nt(vc, g_bd)
        ds = (p * (dp - jnp.sum(p * dp, axis=0, keepdims=True))).astype(BF)
        gqkv[rows, pl.ds(at, 128)] = (gather(tn(ds, kc)) * HEAD_SCALE).astype(BF)
        gqkv[rows, pl.ds(pl.multiple_of(at + 768, 128), 128)] = (nn(ds, q_bd) * HEAD_SCALE).astype(BF)
        gqkv[rows, pl.ds(pl.multiple_of(at + 1536, 128), 128)] = nn(pb, g_bd).astype(BF)
        return carry

    lax.fori_loop(0, 24, attend, 0)

    for n in range(3):
        cols = slice(n * 256, (n + 1) * 256)
        work[:, cols] = nt(gqkv[...], wqkv[cols, :]).astype(BF)
    permute(perm_arr, work, g0)
    exchange(peer_a, me_a, g0, g1, 4, True)
    for n in range(3):
        cols = slice(n * 256, (n + 1) * 256)
        work2[:, cols] = nn(att[...], wo[:, cols]).astype(BF)
    permute(perm_arr, work2, m0)
    exchange(peer_a, me_a, m0, m1, 5, True)

    def outer(n, carry):
        cols = pl.ds(pl.multiple_of(n * 384, 128), 384)
        got = tn(cot_g[:, cols], att[...]).astype(BF)
        gp0[pl.ds(2 * n, 2)] = got.reshape(2, 4, 48, D)
        return carry

    lax.fori_loop(0, 2, outer, 0)

    def gp_y(d, sends):
        k = (y + d) % 4
        copy = pltpu.make_async_remote_copy(
            src_ref=gp0.at[:, k], dst_ref=gp1.at[y] if sends else gp1.at[k],
            send_sem=gpy_s.at[d], recv_sem=gpy_r.at[y if sends else k],
            device_id=device(x, k, z, c), device_id_type=MESH,
        )
        copy.start() if sends else copy.wait()

    def gp_z(d, sends):
        k = (zl + d) % 4
        copy = pltpu.make_async_remote_copy(
            src_ref=gp2.at[k], dst_ref=gp3.at[zl] if sends else gp3.at[k],
            send_sem=gpz_s.at[d], recv_sem=gpz_r.at[zl if sends else k],
            device_id=device(x, y, zh * 4 + k, c), device_id_type=MESH,
        )
        copy.start() if sends else copy.wait()

    def gp_l(d, sends):
        k = (a + d) % 8
        copy = pltpu.make_async_remote_copy(
            src_ref=gp6.at[k], dst_ref=gp7.at[a] if sends else gp7.at[k],
            send_sem=gpl_s.at[d], recv_sem=gpl_r.at[a if sends else k],
            device_id=(k, b), device_id_type=MESH,
        )
        copy.start() if sends else copy.wait()

    for d in range(1, 4):
        gp_y(d, True)
    for k in range(4):
        gp1[y, k] = gp0[k, y]

    exchange(peer_a, me_a, g0, g1, 4, False)
    permute(perm_swap, g1, g2)
    exchange(peer_b, me_b, g2, g3, 6, True)
    exchange(peer_a, me_a, m0, m1, 5, False)
    permute(perm_swap, m1, m2)
    exchange(peer_b, me_b, m2, m3, 7, True)

    exchange(peer_b, me_b, g2, g3, 6, False)
    permute(perm_home, g3, work)
    acc[...] = jnp.zeros_like(acc)

    def norm_back(l, carry):
        ng = work[pl.ds(pl.multiple_of(l * 32, 32), 32), :].astype(F32)
        xh = xhat[l]
        prod = ng * xh
        acc[9] += jnp.sum(prod.reshape(4, 8, D), axis=0)
        u = ng * gain_row
        mu = jnp.mean(u, axis=-1, keepdims=True)
        mux = jnp.mean(prod * gain_row, axis=-1, keepdims=True)
        gh = cot[l].astype(F32) + rstd[l] * (u - mu - xh * mux)
        normed_w[l] = gh.astype(BF)
        return carry

    lax.fori_loop(0, 8, norm_back, 0)
    fill_edges(normed_w, edges_g)
    halos = halo_copies(normed_w, edges_g, rows_in_g, cols_in_g, halo_gs, halo_gr)
    for copy in halos:
        copy.start()

    def tap_sums(l, carry):
        gh = normed_w[l].astype(F32)
        for i in range(3):
            for j in range(3):
                acc[3 * i + j] += jnp.sum((shifted[j, l + i] * gh).reshape(4, 8, D), axis=0)
        return carry

    lax.fori_loop(0, 8, tap_sums, 0)
    for k in range(16):
        if k < 10:
            s0[k] = jnp.sum(acc[k], axis=0, keepdims=True)
        else:
            s0[k] = jnp.zeros((1, D), F32)

    def sums(peer, me, src, dst, slot, whole_src, sends):
        def step(d, carry):
            k = (me + d) % 16
            copy = pltpu.make_async_remote_copy(
                src_ref=src if whole_src else src.at[k], dst_ref=dst.at[me] if sends else dst.at[k],
                send_sem=sum_s.at[slot, d], recv_sem=sum_r.at[slot, me if sends else k],
                device_id=peer(k), device_id_type=MESH,
            )
            if sends:
                copy.start()
            else:
                copy.wait()
            return carry

        lax.fori_loop(1, 16, step, 0)
        if sends:
            dst[me] = src[...] if whole_src else src[me]

    sums(peer_a, me_a, s0, s1, 0, False, True)

    for d in range(1, 4):
        gp_y(d, False)
    for k in range(4):
        total = gp1[0, k].astype(F32)
        for i in range(1, 4):
            total = total + gp1[i, k].astype(F32)
        gp2[k] = total.astype(BF)
    for d in range(1, 4):
        gp_z(d, True)
    gp3[zl] = gp2[zl]

    sums(peer_a, me_a, s0, s1, 0, False, False)
    s2[...] = jnp.sum(s1[...], axis=0)
    sums(peer_b, me_b, s2, s3, 1, True, True)

    exchange(peer_b, me_b, m2, m3, 7, False)
    permute(perm_home, m3, work2)
    for l in range(8):
        block_out[l] = (hid[l].astype(F32) + work2[l * 32 : (l + 1) * 32, :].astype(F32)).astype(BF)

    for copy in halos:
        copy.wait()
    fill_shifted(normed_w, rows_in_g, cols_in_g)

    for d in range(1, 4):
        gp_z(d, False)
    total = gp3[0].astype(F32)
    for i in range(1, 4):
        total = total + gp3[i].astype(F32)
    gp4[...] = total.reshape(2, 24, D)
    core = pltpu.make_async_remote_copy(
        src_ref=gp4.at[1 - c], dst_ref=gp5, send_sem=gpc_s, recv_sem=gpc_r,
        device_id=device(x, y, z, 1 - c), device_id_type=MESH,
    )
    core.start()

    sums(peer_b, me_b, s2, s3, 1, True, False)
    s4[...] = jnp.sum(s3[...], axis=0) * TOTAL_SCALE
    sums(peer_a, me_a, s4, sums_out, 2, True, True)

    def grad_row(l, carry):
        grad_fields[l] = conv_row(l, True).astype(BF)
        return carry

    lax.fori_loop(0, 4, grad_row, 0)
    core.wait()
    total = gp4[c] + gp5[...]
    for i in range(8):
        gp6[i, :, 0:96] = total[:, i * 96 : (i + 1) * 96]
        gp6[i, :, 96:128] = jnp.zeros((24, 32), F32)
    for d in range(1, 8):
        gp_l(d, True)
    gp7[a] = gp6[a]
    lax.fori_loop(4, 8, grad_row, 0)

    for d in range(1, 8):
        gp_l(d, False)
    gp_out[...] = jnp.sum(gp7[...], axis=0) * TOTAL_SCALE
    sums(peer_a, me_a, s4, sums_out, 2, True, False)


def body(
    fields, conv_kernel, layer_norm_gain, qkv_weight, out_weight, score_bias, pattern, cotangent
):
    vm = pl.BlockSpec(memory_space=pltpu.VMEM)
    hbm = pl.BlockSpec(memory_space=pl.ANY)
    dma = pltpu.SemaphoreType.DMA

    def vmem(shape, dtype):
        return pltpu.VMEM(shape, dtype)

    scratch = (
        [vmem((D, 3 * D), BF), vmem((D, D), BF), vmem((24, 64, 64), F32), vmem((6, 64, 256), F32), dma((3,))]
        + [vmem((2, 8, D), BF), vmem((2, 8, D), BF)]
        + [vmem((2, 32, D), BF), vmem((6, 8, D), BF)] * 2
        + [dma((8,))] * 4
        + [vmem((3, 10, 32, D), F32), vmem((8, 32, D), BF), vmem((8, 32, D), F32), vmem((8, 32, 1), F32)]
        + [vmem((256, D), BF)] * 2
        + [vmem((8, 32, D), BF)]
        + [vmem((256, 256), BF)] * 5
        + [vmem((16, 16, D), BF)] * 16
        + [dma((8, 16)), dma((8, 16))]
        + [vmem((256, D), BF), vmem((256, D), BF), vmem((256, 3 * D), BF), vmem((256, D), BF), vmem((256, D), BF), vmem((256, 3 * D), BF)]
        + [vmem((4, 4, 48, D), BF), vmem((4, 4, 48, D), BF), vmem((4, 48, D), BF), vmem((4, 48, D), BF)]
        + [vmem((2, 24, D), F32), vmem((24, D), F32), vmem((8, 24, 128), F32), vmem((8, 24, 128), F32)]
        + [dma((4,)), dma((4,)), dma((4,)), dma((4,)), dma(()), dma(()), dma((8,)), dma((8,))]
        + [vmem((10, 8, D), F32), vmem((16, 1, D), F32), vmem((16, 1, D), F32), vmem((1, D), F32), vmem((16, 1, D), F32), vmem((1, D), F32)]
        + [dma((3, 16)), dma((3, 16))]
    )
    block_out, grad_fields, gp, sums = pl.pallas_call(
        kernel,
        out_shape=(
            jax.ShapeDtypeStruct((8, 32, D), BF),
            jax.ShapeDtypeStruct((8, 32, D), BF),
            jax.ShapeDtypeStruct((24, 128), F32),
            jax.ShapeDtypeStruct((16, 1, D), F32),
        ),
        in_specs=[vm] * 5 + [hbm] * 3,
        out_specs=(vm,) * 4,
        scratch_shapes=scratch,
        name="section",
        compiler_params=pltpu.CompilerParams(
            collective_id=0, has_side_effects=True, vmem_limit_bytes=60 << 20
        ),
    )(
        fields, cotangent, conv_kernel.reshape(9, D), layer_norm_gain.reshape(1, D),
        pattern.reshape(1, 256), qkv_weight, out_weight, score_bias,
    )
    return (
        block_out,
        grad_fields,
        jnp.transpose(gp[:, :96]),
        sums[:9, 0, :].reshape(3, 3, D),
        sums[9, 0, :],
    )


def solution(mesh):
    split = P("lat", "lon", None)
    return jax.shard_map(
        body,
        mesh=mesh,
        in_specs=(split, P(), P(), P(), P(), P(), split, split),
        out_specs=(split, split, P("lat", "lon"), P(), P()),
        check_vma=False,
    )
```

time: 638 us -> 131 us (0.21); the launches traced: 629 us -> 131 us
  waiting for transfers between devices: 307 us -> 0 us
  Pallas kernels: 0 us -> 120 us
  blocking collectives: 92.7 us -> 0 us
  starting transfers between devices: 73.1 us -> 0 us
  local copies, waits for them, and re-layouts: 80.9 us -> 10.2 us
  other arithmetic: 39.4 us -> 0 us
  matrix products: 20.8 us -> 0 us
  between operations: 15.6 us -> 0.65 us
    unnamed x3 -> x0, waiting for transfers between devices: 253 us -> none
    pallas_call x0 -> x1, Pallas kernels: none -> 120 us  [body(): pl.pallas_call(kernel, out_shape=(jax.ShapeDtypeStruct((8, 32, D), BF), j...]
    psum x1 -> x0, blocking collectives: 77.1 us -> none  [body(): lax.psum((gain_on_device, kernel_local), ('lat', 'lon'))]
    all_to_all x7 -> x0, starting transfers between devices: 53.8 us -> none  [the longest x2 22.7 us: to_owner(): lax.all_to_all(lax.all_to_all(packed, 'lat', split_axis=0, concat_axis=3,...]
    all_to_all x7 -> x0, waiting for transfers between devices: 42.8 us -> none  [the longest x2 14.5 us: to_owner(): lax.all_to_all(lax.all_to_all(packed, 'lat', split_axis=0, concat_axis=3,...]
    dot_general x11 -> x0, matrix products: 20.8 us -> none  [the longest x1 3.18 us: body(): jnp.einsum('gihd,gjhd->ghij', grad_heads, value_rows, preferred_element_t...]
    ppermute x8 -> x0, starting transfers between devices: 19 us -> none  [the longest x4 15.3 us: extended(): before = lax.ppermute(last, axis, up)]
    all_to_all x1 -> x0, blocking collectives: 15.7 us -> none  [to_owner(): lax.all_to_all(packed, 'lat', split_axis=0, concat_axis=3, tiled=True)]
  transfers between devices with their start and end apart: 17 -> 0, of which waited for: 9 -> 0; matrix products, arithmetic and copies ran while one was open for 15% -> 0% of each run, Pallas kernels for 0% -> 0%
where the time goes in v1:
time: 131 us
  Pallas kernels  120 us (92%)
  local copies, waits for them, and re-layouts  10.2 us (8%)
    pallas_call x1, Pallas kernels, body(): pl.pallas_call(kernel, out_shape=(jax.ShapeDtypeStruct((8, 32, D), BF), j...  120 us
    unnamed x2, local copies, waits for them, and re-layouts  3.53 us

profile of v1, /device:TPU:1, one launch (start us, length us, event | category | flops | bytes accessed | tf_op | source)
XLA Modules:
  0.0 130.7 jit_solution(16065424287527108290)
XLA Ops:
  0.6 1.4 %reshape.19.taps = f32[9,768]{1,0:T(8,128)} reshape(f32[3,3,768]{2,1,0:T(4,128)} %param.9) | data formatting | bytes 55296 | tf_op jit(solution)/shard_map/reshape | solution.py:515
  2.0 1.3 reshape.20.gain
  3.3 119.8 %section.1 = (bf16[8,32,768]{2,1,0:T(8,128)(2,1)}, bf16[8,32,768]{2,1,0:T(8,128)(2,1)}, f32[24,128]{1,0:T(8,128)}, f32[16,1,768]{2,1,0:T(1,128)}) custom-call(bf16[8,32,768]{2,1,0:T(8,128)(2,1)} %fields.1, bf16[8,32,768]{2,1,0:T(8,128)(2,1)} %cot.1, f32[9,768]{1,0:T(8,128)} %reshape.19.taps, f32[1,768]{1,0:T(1,128)} %reshape.20.gain, s32[1,256]{1,0:T(1,128)} %bitcast.3, ...), custom_call_target="tpu_custom_call" | custom-call | tf_op jit(solution)/shard_map/section/pallas_call | solution.py:499
  123.1 0.8 slice_reduce_fusion
  123.9 0.6 reshape_squeeze.3
  124.6 1.3 slice_reduce_fusion.1
  125.8 1.3 slice_bitcast_fusion
  127.2 1.8 %copy.16 = bf16[8,32,768]{2,1,0:T(8,128)(2,1)} copy(bf16[8,32,768]{2,1,0:T(8,128)(2,1)} %get-tuple-element.18) | data formatting | bytes 786432
  128.9 1.8 %copy.17 = bf16[8,32,768]{2,1,0:T(8,128)(2,1)} copy(bf16[8,32,768]{2,1,0:T(8,128)(2,1)} %get-tuple-element.19) | data formatting | bytes 786432

commit v2 on v1

--- a/solution.py
+++ b/solution.py
@@ -28,8 +28,16 @@
     return lax.dot_general(a, b, (((0,), (0,)), ((), ())), preferred_element_type=F32)
 
 
+def div(a, n):
+    return lax.div(a, jnp.int32(n))
+
+
+def rem(a, n):
+    return lax.rem(a, jnp.int32(n))
+
+
 def device(x, y, z, c):
-    return (x * 2 + z // 4, (z % 4) * 8 + y * 2 + c)
+    return (x * 2 + div(z, 4), rem(z, 4) * 8 + y * 2 + c)
 
 
 def one_hot(cond):
@@ -52,32 +60,32 @@
 
 def kernel(
     fields, cot, taps, gain, pat, wqkv_hbm, wo_hbm, bias_hbm,
-    block_out, grad_fields, gp_out, sums_out,
+    block_out, grad_fields, gp_out, taps_out, gain_out,
     wqkv, wo, bias, bias_t, w_sem,
     edges, edges_g, rows_in, cols_in, rows_in_g, cols_in_g, halo_s, halo_r, halo_gs, halo_gr,
     shifted, hid, xhat, rstd, work, work2, normed_w,
     perm_out, perm_home, perm_swap, perm_pos, perm_arr,
     c0, c1, c2, c3, n0, n1, n2, n3, g0, g1, g2, g3, m0, m1, m2, m3, a2a_s, a2a_r,
-    cot_g, nrm_g, qkv, grad_att, att, gqkv,
+    probs, cot_g, nrm_g, qkv, grad_att, att, gqkv,
     gp0, gp1, gp2, gp3, gp4, gp5, gp6, gp7, gpy_s, gpy_r, gpz_s, gpz_r, gpc_s, gpc_r, gpl_s, gpl_r,
-    acc, s0, s1, s2, s3, s4, sum_s, sum_r,
+    acc, s0, s1, s2, s3, s4, s5, sum_s, sum_r,
 ):
     a = lax.axis_index("lat")
     b = lax.axis_index("lon")
-    x, zh = a // 2, a % 2
-    zl, y, c = b // 8, (b // 2) % 4, b % 2
+    x, zh = div(a, 2), rem(a, 2)
+    zl, y, c = div(b, 8), rem(div(b, 2), 4), rem(b, 2)
     z = zh * 4 + zl
     me_b = x * 4 + y
     me_a = z * 2 + c
 
     def peer_b(k):
-        return device(k // 4, k % 4, z, c)
+        return device(div(k, 4), rem(k, 4), z, c)
 
     def peer_a(k):
-        return device(x, y, k // 2, k % 2)
+        return device(x, y, div(k, 2), rem(k, 2))
 
     def neighbour(da, db):
-        return ((a + da + 8) % 8, (b + db + 32) % 32)
+        return (rem(a + da + 8, 8), rem(b + db + 32, 32))
 
     loads = [
         pltpu.make_async_copy(wqkv_hbm, wqkv, w_sem.at[0]),
@@ -90,8 +98,8 @@
     bar = pltpu.get_barrier_semaphore()
 
     def greet(d, carry):
-        pl.semaphore_signal(bar, inc=1, device_id=peer_b((me_b + d) % 16), device_id_type=MESH)
-        pl.semaphore_signal(bar, inc=1, device_id=peer_a((me_a + d) % 16), device_id_type=MESH)
+        pl.semaphore_signal(bar, inc=1, device_id=peer_b(rem(me_b + d, 16)), device_id_type=MESH)
+        pl.semaphore_signal(bar, inc=1, device_id=peer_a(rem(me_a + d, 16)), device_id_type=MESH)
         return carry
 
     offsets = [(-1, 0), (1, 0), (0, -1), (0, 1), (-1, -1), (-1, 1), (1, -1), (1, 1)]
@@ -99,7 +107,7 @@
         pl.semaphore_signal(bar, inc=1, device_id=neighbour(da, db), device_id_type=MESH)
     for d in range(1, 4):
         pl.semaphore_signal(
-            bar, inc=1, device_id=device((x + d) % 4, y, (z + 4) % 8, c), device_id_type=MESH
+            bar, inc=1, device_id=device(rem(x + d, 4), y, rem(z + 4, 8), c), device_id_type=MESH
         )
     lax.fori_loop(1, 16, greet, 0)
 
@@ -156,7 +164,7 @@
 
     def exchange(peer, me, src, dst, slot, sends):
         def step(d, carry):
-            k = (me + d) % 16
+            k = rem(me + d, 16)
             copy = pltpu.make_async_remote_copy(
                 src_ref=src.at[k], dst_ref=dst.at[me] if sends else dst.at[k],
                 send_sem=a2a_s.at[slot, d], recv_sem=a2a_r.at[slot, me if sends else k],
@@ -179,6 +187,17 @@
             got = nn(perm[...], rows).astype(BF)
             dst[..., cols] = got.reshape(dst.shape[:-1] + (256,))
 
+    def permute_out(perm, src, dst, half):
+        rows = src[..., half * 384 : (half + 1) * 384].reshape(256, 384)
+        dst[half] = nn(perm[...], rows).astype(BF).reshape(16, 16, 384)
+
+    def permute_mid(src, dst, half):
+        dst[half] = nn(perm_swap[...], src[half].reshape(256, 384)).astype(BF).reshape(16, 16, 384)
+
+    def permute_in(perm, src, dst, half):
+        got = nn(perm[...], src[half].reshape(256, 384)).astype(BF)
+        dst[:, half * 384 : (half + 1) * 384] = got
+
     pat_hot = one_hot(iota2(0) == pat[...])
     order_hot = one_hot(iota2(0) == slot_order(iota2(1)))
     perm_out[...] = nt(order_hot, pat_hot).astype(BF)
@@ -187,14 +206,16 @@
     perm_pos[...] = one_hot(iota2(1) == arrival_order(iota2(0)))
     perm_arr[...] = one_hot(iota2(0) == arrival_order(iota2(1)))
     fill_edges(fields, edges)
-    permute(perm_out, cot, c0)
+    permute_out(perm_out, cot, c0, 0)
+    permute_out(perm_out, cot, c0, 1)
 
     pl.semaphore_wait(bar, 41)
 
     halos = halo_copies(fields, edges, rows_in, cols_in, halo_s, halo_r)
     for copy in halos:
         copy.start()
-    exchange(peer_b, me_b, c0, c1, 0, True)
+    exchange(peer_b, me_b, c0.at[0], c1.at[0], 0, True)
+    exchange(peer_b, me_b, c0.at[1], c1.at[1], 1, True)
 
     loads[2].wait()
     for q in range(6):
@@ -203,14 +224,14 @@
     for copy in halos:
         copy.wait()
     fill_shifted(fields, rows_in, cols_in)
-    gain_row = gain[...]
+    gain_row = gain[...].reshape(1, D)
 
     def conv_row(l, flip):
         out = shifted[1, l + 1]
         for i in range(3):
             for j in range(3):
-                t = 8 - (3 * i + j) if flip else 3 * i + j
-                out = out + taps[t : t + 1, :] * shifted[j, l + i]
+                ti, tj = (2 - i, 2 - j) if flip else (i, j)
+                out = out + taps[ti, tj : tj + 1, :] * shifted[j, l + i]
         return out
 
     def norm_row(l, carry):
@@ -228,24 +249,28 @@
         return carry
 
     lax.fori_loop(0, 8, norm_row, 0)
-    permute(perm_out, normed_w, n0)
-    exchange(peer_b, me_b, n0, n1, 1, True)
-
-    exchange(peer_b, me_b, c0, c1, 0, False)
-    permute(perm_swap, c1, c2)
-    exchange(peer_a, me_a, c2, c3, 2, True)
-    exchange(peer_b, me_b, n0, n1, 1, False)
-    permute(perm_swap, n1, n2)
-    exchange(peer_a, me_a, n2, n3, 3, True)
-
-    exchange(peer_a, me_a, c2, c3, 2, False)
-    permute(perm_pos, c3, cot_g)
-    loads[1].wait()
-    for n in range(3):
-        cols = slice(n * 256, (n + 1) * 256)
-        grad_att[:, cols] = nt(cot_g[...], wo[cols, :]).astype(BF)
-    exchange(peer_a, me_a, n2, n3, 3, False)
-    permute(perm_pos, n3, nrm_g)
+    permute_out(perm_out, normed_w, n0, 0)
+    exchange(peer_b, me_b, n0.at[0], n1.at[0], 2, True)
+    permute_out(perm_out, normed_w, n0, 1)
+    exchange(peer_b, me_b, n0.at[1], n1.at[1], 3, True)
+
+    exchange(peer_b, me_b, c0.at[0], c1.at[0], 0, False)
+    permute_mid(c1, c2, 0)
+    exchange(peer_a, me_a, c2.at[0], c3.at[0], 4, True)
+    exchange(peer_b, me_b, c0.at[1], c1.at[1], 1, False)
+    permute_mid(c1, c2, 1)
+    exchange(peer_b, me_b, n0.at[0], n1.at[0], 2, False)
+    permute_mid(n1, n2, 0)
+    exchange(peer_a, me_a, n2.at[0], n3.at[0], 6, True)
+    exchange(peer_b, me_b, n0.at[1], n1.at[1], 3, False)
+    permute_mid(n1, n2, 1)
+    exchange(peer_a, me_a, n2.at[1], n3.at[1], 7, True)
+    exchange(peer_a, me_a, c2.at[1], c3.at[1], 5, True)
+
+    exchange(peer_a, me_a, n2.at[0], n3.at[0], 6, False)
+    permute_in(perm_pos, n3, nrm_g, 0)
+    exchange(peer_a, me_a, n2.at[1], n3.at[1], 7, False)
+    permute_in(perm_pos, n3, nrm_g, 1)
     loads[0].wait()
 
     def project(n, carry):
@@ -269,40 +294,46 @@
             out = jnp.where(lane_head == e, v[e * 64 : (e + 1) * 64, :], out)
         return out
 
-    def attend(u, carry):
-        q = u % 6
-        rows = pl.ds(pl.multiple_of((u // 6) * 64, 64), 64)
-        at = pl.multiple_of(q * 128, 128)
-        qc = qkv[rows, pl.ds(at, 128)]
-        kc = qkv[rows, pl.ds(pl.multiple_of(at + 768, 128), 128)]
-        vc = qkv[rows, pl.ds(pl.multiple_of(at + 1536, 128), 128)]
-        gc = grad_att[rows, pl.ds(at, 128)]
-        q_bd = spread(qc)
-        g_bd = spread(gc)
-        st = nt(kc, q_bd) * HEAD_SCALE + bias_t[q]
-        e = jnp.exp(st - jnp.max(st, axis=0, keepdims=True))
-        p = e * (1.0 / jnp.sum(e, axis=0, keepdims=True))
-        pb = p.astype(BF)
-        att[rows, pl.ds(at, 128)] = gather(tn(pb, vc)).astype(BF)
-        dp = nt(vc, g_bd)
-        ds = (p * (dp - jnp.sum(p * dp, axis=0, keepdims=True))).astype(BF)
-        gqkv[rows, pl.ds(at, 128)] = (gather(tn(ds, kc)) * HEAD_SCALE).astype(BF)
-        gqkv[rows, pl.ds(pl.multiple_of(at + 768, 128), 128)] = (nn(ds, q_bd) * HEAD_SCALE).astype(BF)
-        gqkv[rows, pl.ds(pl.multiple_of(at + 1536, 128), 128)] = nn(pb, g_bd).astype(BF)
-        return carry
-
-    lax.fori_loop(0, 24, attend, 0)
-
-    for n in range(3):
-        cols = slice(n * 256, (n + 1) * 256)
-        work[:, cols] = nt(gqkv[...], wqkv[cols, :]).astype(BF)
-    permute(perm_arr, work, g0)
-    exchange(peer_a, me_a, g0, g1, 4, True)
+    def columns(q, part):
+        return pl.ds(pl.multiple_of(q * 128 + part * D, 128), 128)
+
+    def attend(q, carry):
+        for g in range(4):
+            rows = slice(g * 64, (g + 1) * 64)
+            q_bd = spread(qkv[rows, columns(q, 0)])
+            st = nt(qkv[rows, columns(q, 1)], q_bd) * HEAD_SCALE + bias_t[q]
+            e = jnp.exp(st - jnp.max(st, axis=0, keepdims=True))
+            p = e * (1.0 / jnp.sum(e, axis=0, keepdims=True))
+            probs[q, g] = p
+            att[rows, columns(q, 0)] = gather(tn(p.astype(BF), qkv[rows, columns(q, 2)])).astype(BF)
+        return carry
+
+    def attend_back(q, carry):
+        for g in range(4):
+            rows = slice(g * 64, (g + 1) * 64)
+            q_bd = spread(qkv[rows, columns(q, 0)])
+            g_bd = spread(grad_att[rows, columns(q, 0)])
+            p = probs[q, g]
+            dp = nt(qkv[rows, columns(q, 2)], g_bd)
+            ds = (p * (dp - jnp.sum(p * dp, axis=0, keepdims=True))).astype(BF)
+            dq = gather(tn(ds, qkv[rows, columns(q, 1)])) * HEAD_SCALE
+            gqkv[rows, columns(q, 0)] = dq.astype(BF)
+            gqkv[rows, columns(q, 1)] = (nn(ds, q_bd) * HEAD_SCALE).astype(BF)
+            gqkv[rows, columns(q, 2)] = nn(p.astype(BF), g_bd).astype(BF)
+        return carry
+
+    lax.fori_loop(0, 6, attend, 0)
+
+    loads[1].wait()
     for n in range(3):
         cols = slice(n * 256, (n + 1) * 256)
         work2[:, cols] = nn(att[...], wo[:, cols]).astype(BF)
     permute(perm_arr, work2, m0)
-    exchange(peer_a, me_a, m0, m1, 5, True)
+    exchange(peer_a, me_a, m0, m1, 8, True)
+
+    for h in range(2):
+        exchange(peer_a, me_a, c2.at[h], c3.at[h], 4 + h, False)
+        permute_in(perm_pos, c3, cot_g, h)
 
     def outer(n, carry):
         cols = pl.ds(pl.multiple_of(n * 384, 128), 384)
@@ -313,7 +344,7 @@
     lax.fori_loop(0, 2, outer, 0)
 
     def gp_y(d, sends):
-        k = (y + d) % 4
+        k = rem(y + d, 4)
         copy = pltpu.make_async_remote_copy(
             src_ref=gp0.at[:, k], dst_ref=gp1.at[y] if sends else gp1.at[k],
             send_sem=gpy_s.at[d], recv_sem=gpy_r.at[y if sends else k],
@@ -322,16 +353,16 @@
         copy.start() if sends else copy.wait()
 
     def gp_z(d, sends):
-        k = (zl + d) % 4
+        k = rem(zl + d, 4)
         copy = pltpu.make_async_remote_copy(
-            src_ref=gp2.at[k], dst_ref=gp3.at[zl] if sends else gp3.at[k],
+            src_ref=gp3.at[k], dst_ref=gp4.at[zl] if sends else gp4.at[k],
             send_sem=gpz_s.at[d], recv_sem=gpz_r.at[zl if sends else k],
             device_id=device(x, y, zh * 4 + k, c), device_id_type=MESH,
         )
         copy.start() if sends else copy.wait()
 
     def gp_l(d, sends):
-        k = (a + d) % 8
+        k = rem(a + d, 8)
         copy = pltpu.make_async_remote_copy(
             src_ref=gp6.at[k], dst_ref=gp7.at[a] if sends else gp7.at[k],
             send_sem=gpl_s.at[d], recv_sem=gpl_r.at[a if sends else k],
@@ -344,15 +375,57 @@
     for k in range(4):
         gp1[y, k] = gp0[k, y]
 
-    exchange(peer_a, me_a, g0, g1, 4, False)
-    permute(perm_swap, g1, g2)
-    exchange(peer_b, me_b, g2, g3, 6, True)
-    exchange(peer_a, me_a, m0, m1, 5, False)
+    for n in range(3):
+        cols = slice(n * 256, (n + 1) * 256)
+        grad_att[:, cols] = nt(cot_g[...], wo[cols, :]).astype(BF)
+
+    lax.fori_loop(0, 3, attend_back, 0)
+    exchange(peer_a, me_a, m0, m1, 8, False)
     permute(perm_swap, m1, m2)
-    exchange(peer_b, me_b, m2, m3, 7, True)
-
-    exchange(peer_b, me_b, g2, g3, 6, False)
-    permute(perm_home, g3, work)
+    exchange(peer_b, me_b, m2, m3, 9, True)
+    lax.fori_loop(3, 6, attend_back, 0)
+
+    for half in range(2):
+        for n in range(3 * half, 3 * half + 3):
+            cols = slice(n * 128, (n + 1) * 128)
+            work[:, cols] = nt(gqkv[...], wqkv[cols, :]).astype(BF)
+        permute_out(perm_arr, work, g0, half)
+        exchange(peer_a, me_a, g0.at[half], g1.at[half], 10 + half, True)
+
+    for d in range(1, 4):
+        gp_y(d, False)
+    for k in range(4):
+        total = gp1[0, k].astype(F32)
+        for i in range(1, 4):
+            total = total + gp1[i, k].astype(F32)
+        gp2[0, k] = total[0:24]
+        gp2[1, k] = total[24:48]
+    core = pltpu.make_async_remote_copy(
+        src_ref=gp2.at[1 - c], dst_ref=gp5, send_sem=gpc_s, recv_sem=gpc_r,
+        device_id=device(x, y, z, 1 - c), device_id_type=MESH,
+    )
+    core.start()
+
+    for half in range(2):
+        exchange(peer_a, me_a, g0.at[half], g1.at[half], 10 + half, False)
+        permute_mid(g1, g2, half)
+        exchange(peer_b, me_b, g2.at[half], g3.at[half], 12 + half, True)
+
+    core.wait()
+    for k in range(4):
+        gp3[k] = (gp2[c, k] + gp5[k]).astype(BF)
+    for d in range(1, 4):
+        gp_z(d, True)
+    gp4[zl] = gp3[zl]
+
+    exchange(peer_b, me_b, m2, m3, 9, False)
+    permute(perm_home, m3, work2)
+    for l in range(8):
+        block_out[l] = (hid[l].astype(F32) + work2[l * 32 : (l + 1) * 32, :].astype(F32)).astype(BF)
+
+    for half in range(2):
+        exchange(peer_b, me_b, g2.at[half], g3.at[half], 12 + half, False)
+        permute_in(perm_home, g3, work, half)
     acc[...] = jnp.zeros_like(acc)
 
     def norm_back(l, carry):
@@ -389,7 +462,7 @@
 
     def sums(peer, me, src, dst, slot, whole_src, sends):
         def step(d, carry):
-            k = (me + d) % 16
+            k = rem(me + d, 16)
             copy = pltpu.make_async_remote_copy(
                 src_ref=src if whole_src else src.at[k], dst_ref=dst.at[me] if sends else dst.at[k],
                 send_sem=sum_s.at[slot, d], recv_sem=sum_r.at[slot, me if sends else k],
@@ -408,64 +481,46 @@
     sums(peer_a, me_a, s0, s1, 0, False, True)
 
     for d in range(1, 4):
-        gp_y(d, False)
-    for k in range(4):
-        total = gp1[0, k].astype(F32)
-        for i in range(1, 4):
-            total = total + gp1[i, k].astype(F32)
-        gp2[k] = total.astype(BF)
-    for d in range(1, 4):
-        gp_z(d, True)
-    gp3[zl] = gp2[zl]
-
-    sums(peer_a, me_a, s0, s1, 0, False, False)
-    s2[...] = jnp.sum(s1[...], axis=0)
-    sums(peer_b, me_b, s2, s3, 1, True, True)
-
-    exchange(peer_b, me_b, m2, m3, 7, False)
-    permute(perm_home, m3, work2)
-    for l in range(8):
-        block_out[l] = (hid[l].astype(F32) + work2[l * 32 : (l + 1) * 32, :].astype(F32)).astype(BF)
-
-    for copy in halos:
-        copy.wait()
-    fill_shifted(normed_w, rows_in_g, cols_in_g)
-
-    for d in range(1, 4):
         gp_z(d, False)
-    total = gp3[0].astype(F32)
+    total = gp4[0].astype(F32)
     for i in range(1, 4):
-        total = total + gp3[i].astype(F32)
-    gp4[...] = total.reshape(2, 24, D)
-    core = pltpu.make_async_remote_copy(
-        src_ref=gp4.at[1 - c], dst_ref=gp5, send_sem=gpc_s, recv_sem=gpc_r,
-        device_id=device(x, y, z, 1 - c), device_id_type=MESH,
-    )
-    core.start()
-
-    sums(peer_b, me_b, s2, s3, 1, True, False)
-    s4[...] = jnp.sum(s3[...], axis=0) * TOTAL_SCALE
-    sums(peer_a, me_a, s4, sums_out, 2, True, True)
-
-    def grad_row(l, carry):
-        grad_fields[l] = conv_row(l, True).astype(BF)
-        return carry
-
-    lax.fori_loop(0, 4, grad_row, 0)
-    core.wait()
-    total = gp4[c] + gp5[...]
+        total = total + gp4[i].astype(F32)
     for i in range(8):
         gp6[i, :, 0:96] = total[:, i * 96 : (i + 1) * 96]
         gp6[i, :, 96:128] = jnp.zeros((24, 32), F32)
     for d in range(1, 8):
         gp_l(d, True)
     gp7[a] = gp6[a]
-    lax.fori_loop(4, 8, grad_row, 0)
+
+    for copy in halos:
+        copy.wait()
+    fill_shifted(normed_w, rows_in_g, cols_in_g)
+
+    def grad_row(l, carry):
+        grad_fields[l] = conv_row(l, True).astype(BF)
+        return carry
+
+    sums(peer_a, me_a, s0, s1, 0, False, False)
+    s2[...] = jnp.sum(s1[...], axis=0)
+    sums(peer_b, me_b, s2, s3, 1, True, True)
+    lax.fori_loop(0, 6, grad_row, 0)
+    sums(peer_b, me_b, s2, s3, 1, True, False)
+    s4[...] = jnp.sum(s3[...], axis=0) * TOTAL_SCALE
+    sums(peer_a, me_a, s4, s5, 2, True, True)
+    lax.fori_loop(6, 8, grad_row, 0)
 
     for d in range(1, 8):
         gp_l(d, False)
-    gp_out[...] = jnp.sum(gp7[...], axis=0) * TOTAL_SCALE
-    sums(peer_a, me_a, s4, sums_out, 2, True, False)
+    gp_out[...] = (jnp.sum(gp7[...], axis=0) * TOTAL_SCALE)[:, 0:96]
+    sums(peer_a, me_a, s4, s5, 2, True, False)
+    for k in range(9):
+        taps_out[k // 3, k % 3 : k % 3 + 1, :] = s5[k]
+    gain_out[...] = s5[9].reshape(D)
+
+
+def hand_over(*refs):
+    for k in range(5):
+        refs[5 + k][...] = refs[k][...]
 
 
 def body(
@@ -487,41 +542,43 @@
         + [vmem((256, D), BF)] * 2
         + [vmem((8, 32, D), BF)]
         + [vmem((256, 256), BF)] * 5
-        + [vmem((16, 16, D), BF)] * 16
-        + [dma((8, 16)), dma((8, 16))]
+        + [vmem((2, 16, 16, D // 2), BF)] * 12
+        + [vmem((16, 16, D), BF)] * 4
+        + [dma((14, 16)), dma((14, 16))]
+        + [vmem((6, 4, 64, 256), F32)]
         + [vmem((256, D), BF), vmem((256, D), BF), vmem((256, 3 * D), BF), vmem((256, D), BF), vmem((256, D), BF), vmem((256, 3 * D), BF)]
-        + [vmem((4, 4, 48, D), BF), vmem((4, 4, 48, D), BF), vmem((4, 48, D), BF), vmem((4, 48, D), BF)]
-        + [vmem((2, 24, D), F32), vmem((24, D), F32), vmem((8, 24, 128), F32), vmem((8, 24, 128), F32)]
+        + [vmem((4, 4, 48, D), BF), vmem((4, 4, 48, D), BF), vmem((2, 4, 24, D), F32)]
+        + [vmem((4, 24, D), BF), vmem((4, 24, D), BF), vmem((4, 24, D), F32)]
+        + [vmem((8, 24, 128), F32), vmem((8, 24, 128), F32)]
         + [dma((4,)), dma((4,)), dma((4,)), dma((4,)), dma(()), dma(()), dma((8,)), dma((8,))]
-        + [vmem((10, 8, D), F32), vmem((16, 1, D), F32), vmem((16, 1, D), F32), vmem((1, D), F32), vmem((16, 1, D), F32), vmem((1, D), F32)]
+        + [vmem((10, 8, D), F32), vmem((16, 1, D), F32), vmem((16, 1, D), F32), vmem((1, D), F32), vmem((16, 1, D), F32), vmem((1, D), F32), vmem((16, 1, D), F32)]
         + [dma((3, 16)), dma((3, 16))]
     )
-    block_out, grad_fields, gp, sums = pl.pallas_call(
+    results = (
+        jax.ShapeDtypeStruct((8, 32, D), BF),
+        jax.ShapeDtypeStruct((8, 32, D), BF),
+        jax.ShapeDtypeStruct((24, 96), F32),
+        jax.ShapeDtypeStruct((3, 3, D), F32),
+        jax.ShapeDtypeStruct((D,), F32),
+    )
+    out = pl.pallas_call(
         kernel,
-        out_shape=(
-            jax.ShapeDtypeStruct((8, 32, D), BF),
-            jax.ShapeDtypeStruct((8, 32, D), BF),
-            jax.ShapeDtypeStruct((24, 128), F32),
-            jax.ShapeDtypeStruct((16, 1, D), F32),
-        ),
+        out_shape=results,
         in_specs=[vm] * 5 + [hbm] * 3,
-        out_specs=(vm,) * 4,
+        out_specs=(vm,) * 5,
         scratch_shapes=scratch,
         name="section",
         compiler_params=pltpu.CompilerParams(
             collective_id=0, has_side_effects=True, vmem_limit_bytes=60 << 20
         ),
     )(
-        fields, cotangent, conv_kernel.reshape(9, D), layer_norm_gain.reshape(1, D),
+        fields, cotangent, conv_kernel, layer_norm_gain,
         pattern.reshape(1, 256), qkv_weight, out_weight, score_bias,
     )
-    return (
-        block_out,
-        grad_fields,
-        jnp.transpose(gp[:, :96]),
-        sums[:9, 0, :].reshape(3, 3, D),
-        sums[9, 0, :],
-    )
+    block_out, grad_fields, gp, taps, gain = pl.pallas_call(
+        hand_over, out_shape=results, in_specs=[vm] * 5, out_specs=(vm,) * 5, name="results"
+    )(*out)
+    return (block_out, grad_fields, jnp.transpose(gp), taps, gain)
 
 
 def solution(mesh):

time: 131 us -> 119 us (0.908)
  local copies, waits for them, and re-layouts: 10.2 us -> 0 us
    unnamed x2 -> x0, local copies, waits for them, and re-layouts: 3.53 us -> none
    reshape x2 -> x0, local copies, waits for them, and re-layouts: 2.67 us -> none  [the longest x1 1.4 us: body(): conv_kernel.reshape(9, D)]
    slice x2 -> x0, local copies, waits for them, and re-layouts: 2.1 us -> none  [the longest x1 1.28 us: body(): sums[9, 0, :]]
    pallas_call x1 -> x2, Pallas kernels: 120 us -> 119 us  [the longest x1 116 us: body(): pl.pallas_call(kernel, out_shape=results, in_specs=[vm] * 5 + [hbm] * 3,...]
where the time goes in v2:
time: 119 us
  Pallas kernels  119 us (100%)
    pallas_call x1, Pallas kernels, body(): pl.pallas_call(kernel, out_shape=results, in_specs=[vm] * 5 + [hbm] * 3,...  116 us

profile of v2, /device:TPU:1, one launch (start us, length us, event | category | flops | bytes accessed | tf_op | source)
XLA Modules:
  0.0 119.2 jit_solution(5598600509855891056)
XLA Ops:
  0.6 116.5 %section.1 = (bf16[8,32,768]{2,1,0:T(8,128)(2,1)}, bf16[8,32,768]{2,1,0:T(8,128)(2,1)}, f32[24,96]{1,0:T(8,128)}, f32[3,3,768]{2,1,0:T(4,128)}, f32[768]{0:T(1024)}) custom-call(bf16[8,32,768]{2,1,0:T(8,128)(2,1)} %fields.1, bf16[8,32,768]{2,1,0:T(8,128)(2,1)} %cot.1, f32[3,3,768]{2,1,0:T(4,128)} %taps.1, f32[768]{0:T(1024)} %gain.1, s32[1,256]{1,0:T(1,128)} %bitcast.2, ...), custom_call_target="tpu_custom_call" | custom-call | tf_op jit(solution)/shard_map/section/pallas_call | solution.py:564
  117.1 2.1 %results.1 = (bf16[8,32,768]{2,1,0:T(8,128)(2,1)}, bf16[8,32,768]{2,1,0:T(8,128)(2,1)}, f32[24,96]{1,0:T(8,128)}, f32[3,3,768]{2,1,0:T(4,128)}, f32[768]{0:T(1024)}) custom-call(bf16[8,32,768]{2,1,0:T(8,128)(2,1)} %get-tuple-element.15.refs_0_, bf16[8,32,768]{2,1,0:T(8,128)(2,1)} %get-tuple-element.16.refs_1_, f32[24,96]{1,0:T(8,128)} %get-tuple-element.17.refs_2_, ...), custom_call_target="tpu_custom_call" | custom-call | tf_op jit(solution)/shard_map/results/pallas_call | solution.py:578

commit v3 on v2

--- a/solution.py
+++ b/solution.py
@@ -59,10 +59,10 @@
 
 
 def kernel(
-    fields, cot, taps, gain, pat, wqkv_hbm, wo_hbm, bias_hbm,
+    fields_hbm, cot_hbm, taps_hbm, gain_hbm, pat_hbm, wqkv_hbm, wo_hbm, bias_hbm,
     block_out, grad_fields, gp_out, taps_out, gain_out,
-    wqkv, wo, bias, bias_t, w_sem,
-    edges, edges_g, rows_in, cols_in, rows_in_g, cols_in_g, halo_s, halo_r, halo_gs, halo_gr,
+    fields, cot, taps, gain, pat, wqkv, wo, bias, bias_t, w_sem,
+    corners, corners_g, corner_in, corner_in_g, edges, edges_g, rows_in, cols_in, rows_in_g, cols_in_g, halo_s, halo_r, halo_gs, halo_gr,
     shifted, hid, xhat, rstd, work, work2, normed_w,
     perm_out, perm_home, perm_swap, perm_pos, perm_arr,
     c0, c1, c2, c3, n0, n1, n2, n3, g0, g1, g2, g3, m0, m1, m2, m3, a2a_s, a2a_r,
@@ -87,13 +87,16 @@
     def neighbour(da, db):
         return (rem(a + da + 8, 8), rem(b + db + 32, 32))
 
-    loads = [
-        pltpu.make_async_copy(wqkv_hbm, wqkv, w_sem.at[0]),
-        pltpu.make_async_copy(wo_hbm, wo, w_sem.at[1]),
-        pltpu.make_async_copy(bias_hbm, bias, w_sem.at[2]),
-    ]
-    for load in loads:
-        load.start()
+    loads = {}
+    for i, (name, src, dst) in enumerate(
+        (
+            ("fields", fields_hbm, fields), ("pat", pat_hbm, pat), ("cot", cot_hbm, cot),
+            ("bias", bias_hbm, bias), ("taps", taps_hbm, taps), ("gain", gain_hbm, gain),
+            ("wqkv", wqkv_hbm, wqkv), ("wo", wo_hbm, wo),
+        )
+    ):
+        loads[name] = pltpu.make_async_copy(src, dst, w_sem.at[i])
+        loads[name].start()
 
     bar = pltpu.get_barrier_semaphore()
 
@@ -114,7 +117,7 @@
     row8 = lax.broadcasted_iota(jnp.int32, (8, D), 0)
     row32 = lax.broadcasted_iota(jnp.int32, (32, D), 0)
 
-    def fill_edges(source, dest):
+    def fill_edges(source, dest, corner):
         left = jnp.zeros((8, D), F32)
         right = jnp.zeros((8, D), F32)
         for l in range(8):
@@ -123,14 +126,18 @@
             right = jnp.where(row8 == l, row[31:32, :], right)
         dest[0] = left.astype(BF)
         dest[1] = right.astype(BF)
-
-    def halo_copies(source, edge, rows, cols, ss, rs):
+        corner[0] = left[0:1].astype(BF)
+        corner[1] = right[0:1].astype(BF)
+        corner[2] = left[7:8].astype(BF)
+        corner[3] = right[7:8].astype(BF)
+
+    def halo_copies(source, edge, corner, rows, cols, corner_to, ss, rs):
         out = []
         routes = [
             (source.at[0], rows.at[1]), (source.at[7], rows.at[0]),
             (edge.at[0], cols.at[1]), (edge.at[1], cols.at[0]),
-            (edge.at[0], cols.at[5]), (edge.at[1], cols.at[4]),
-            (edge.at[0], cols.at[3]), (edge.at[1], cols.at[2]),
+            (corner.at[0], corner_to.at[3]), (corner.at[1], corner_to.at[2]),
+            (corner.at[2], corner_to.at[1]), (corner.at[3], corner_to.at[0]),
         ]
         for m, (src, dst) in enumerate(routes):
             out.append(
@@ -144,16 +151,16 @@
     top_mask = (a > 0).astype(F32)
     bottom_mask = (a < 7).astype(F32)
 
-    def fill_shifted(source, rows, cols):
+    def fill_shifted(source, rows, cols, corner):
         for r in range(10):
             if r == 0:
                 f = rows[0].astype(F32) * top_mask
-                le = cols[2].astype(F32)[7:8, :] * top_mask
-                ri = cols[3].astype(F32)[7:8, :] * top_mask
+                le = corner[0].astype(F32) * top_mask
+                ri = corner[1].astype(F32) * top_mask
             elif r == 9:
                 f = rows[1].astype(F32) * bottom_mask
-                le = cols[4].astype(F32)[0:1, :] * bottom_mask
-                ri = cols[5].astype(F32)[0:1, :] * bottom_mask
+                le = corner[2].astype(F32) * bottom_mask
+                ri = corner[3].astype(F32) * bottom_mask
             else:
                 f = source[r - 1].astype(F32)
                 le = cols[0].astype(F32)[r - 1 : r, :]
@@ -189,41 +196,49 @@
 
     def permute_out(perm, src, dst, half):
         rows = src[..., half * 384 : (half + 1) * 384].reshape(256, 384)
-        dst[half] = nn(perm[...], rows).astype(BF).reshape(16, 16, 384)
+        dst[half] = nn(perm[half], rows).astype(BF).reshape(16, 16, 384)
 
     def permute_mid(src, dst, half):
         dst[half] = nn(perm_swap[...], src[half].reshape(256, 384)).astype(BF).reshape(16, 16, 384)
 
     def permute_in(perm, src, dst, half):
-        got = nn(perm[...], src[half].reshape(256, 384)).astype(BF)
+        got = nn(perm[half], src[half].reshape(256, 384)).astype(BF)
         dst[:, half * 384 : (half + 1) * 384] = got
 
-    pat_hot = one_hot(iota2(0) == pat[...])
-    order_hot = one_hot(iota2(0) == slot_order(iota2(1)))
-    perm_out[...] = nt(order_hot, pat_hot).astype(BF)
-    perm_home[...] = nt(pat_hot, order_hot).astype(BF)
-    perm_swap[...] = one_hot(iota2(1) == (iota2(0) & 15) * 16 + (iota2(0) >> 4))
-    perm_pos[...] = one_hot(iota2(1) == arrival_order(iota2(0)))
-    perm_arr[...] = one_hot(iota2(0) == arrival_order(iota2(1)))
-    fill_edges(fields, edges)
-    permute_out(perm_out, cot, c0, 0)
-    permute_out(perm_out, cot, c0, 1)
-
+    loads["fields"].wait()
+    fill_edges(fields, edges, corners)
     pl.semaphore_wait(bar, 41)
-
-    halos = halo_copies(fields, edges, rows_in, cols_in, halo_s, halo_r)
+    halos = halo_copies(fields, edges, corners, rows_in, cols_in, corner_in, halo_s, halo_r)
     for copy in halos:
         copy.start()
-    exchange(peer_b, me_b, c0.at[0], c1.at[0], 0, True)
-    exchange(peer_b, me_b, c0.at[1], c1.at[1], 1, True)
-
-    loads[2].wait()
+
+    loads["pat"].wait()
+    pat_hot = one_hot(iota2(0) == pat[...])
+    for half, first, second in ((0, slot_order, arrival_order), (1, arrival_order, slot_order)):
+        order_hot = one_hot(iota2(0) == first(iota2(1)))
+        perm_out[half] = nt(order_hot, pat_hot).astype(BF)
+        perm_home[half] = nt(pat_hot, order_hot).astype(BF)
+        perm_pos[half] = one_hot(iota2(1) == second(iota2(0)))
+        perm_arr[half] = one_hot(iota2(0) == second(iota2(1)))
+    perm_swap[...] = one_hot(iota2(1) == (iota2(0) & 15) * 16 + (iota2(0) >> 4))
+    first_peer = ((peer_b, me_b), (peer_a, me_a))
+    second_peer = ((peer_a, me_a), (peer_b, me_b))
+
+    loads["cot"].wait()
+    permute_out(perm_out, cot, c0, 0)
+    exchange(*first_peer[0], c0.at[0], c1.at[0], 4, True)
+    permute_out(perm_out, cot, c0, 1)
+
+    loads["bias"].wait()
     for q in range(6):
         bias_t[q] = jnp.transpose(bias[4 * q : 4 * q + 4].reshape(256, 64))
 
     for copy in halos:
         copy.wait()
-    fill_shifted(fields, rows_in, cols_in)
+    exchange(*first_peer[1], c0.at[1], c1.at[1], 5, True)
+    fill_shifted(fields, rows_in, cols_in, corner_in)
+    loads["taps"].wait()
+    loads["gain"].wait()
     gain_row = gain[...].reshape(1, D)
 
     def conv_row(l, flip):
@@ -249,29 +264,23 @@
         return carry
 
     lax.fori_loop(0, 8, norm_row, 0)
-    permute_out(perm_out, normed_w, n0, 0)
-    exchange(peer_b, me_b, n0.at[0], n1.at[0], 2, True)
-    permute_out(perm_out, normed_w, n0, 1)
-    exchange(peer_b, me_b, n0.at[1], n1.at[1], 3, True)
-
-    exchange(peer_b, me_b, c0.at[0], c1.at[0], 0, False)
-    permute_mid(c1, c2, 0)
-    exchange(peer_a, me_a, c2.at[0], c3.at[0], 4, True)
-    exchange(peer_b, me_b, c0.at[1], c1.at[1], 1, False)
-    permute_mid(c1, c2, 1)
-    exchange(peer_b, me_b, n0.at[0], n1.at[0], 2, False)
-    permute_mid(n1, n2, 0)
-    exchange(peer_a, me_a, n2.at[0], n3.at[0], 6, True)
-    exchange(peer_b, me_b, n0.at[1], n1.at[1], 3, False)
-    permute_mid(n1, n2, 1)
-    exchange(peer_a, me_a, n2.at[1], n3.at[1], 7, True)
-    exchange(peer_a, me_a, c2.at[1], c3.at[1], 5, True)
-
-    exchange(peer_a, me_a, n2.at[0], n3.at[0], 6, False)
-    permute_in(perm_pos, n3, nrm_g, 0)
-    exchange(peer_a, me_a, n2.at[1], n3.at[1], 7, False)
-    permute_in(perm_pos, n3, nrm_g, 1)
-    loads[0].wait()
+    for h in range(2):
+        permute_out(perm_out, normed_w, n0, h)
+        exchange(*first_peer[h], n0.at[h], n1.at[h], h, True)
+    for h in range(2):
+        exchange(*first_peer[h], c0.at[h], c1.at[h], 4 + h, False)
+        permute_mid(c1, c2, h)
+    for h in range(2):
+        exchange(*first_peer[h], n0.at[h], n1.at[h], h, False)
+        permute_mid(n1, n2, h)
+        exchange(*second_peer[h], n2.at[h], n3.at[h], 2 + h, True)
+    for h in range(2):
+        exchange(*second_peer[h], c2.at[h], c3.at[h], 6 + h, True)
+
+    for h in (1, 0):
+        exchange(*second_peer[h], n2.at[h], n3.at[h], 2 + h, False)
+        permute_in(perm_pos, n3, nrm_g, h)
+    loads["wqkv"].wait()
 
     def project(n, carry):
         cols = pl.ds(pl.multiple_of(n * 256, 256), 256)
@@ -324,15 +333,15 @@
 
     lax.fori_loop(0, 6, attend, 0)
 
-    loads[1].wait()
+    loads["wo"].wait()
     for n in range(3):
         cols = slice(n * 256, (n + 1) * 256)
         work2[:, cols] = nn(att[...], wo[:, cols]).astype(BF)
-    permute(perm_arr, work2, m0)
+    permute(perm_arr.at[0], work2, m0)
     exchange(peer_a, me_a, m0, m1, 8, True)
 
     for h in range(2):
-        exchange(peer_a, me_a, c2.at[h], c3.at[h], 4 + h, False)
+        exchange(*second_peer[h], c2.at[h], c3.at[h], 6 + h, False)
         permute_in(perm_pos, c3, cot_g, h)
 
     def outer(n, carry):
@@ -379,18 +388,18 @@
         cols = slice(n * 256, (n + 1) * 256)
         grad_att[:, cols] = nt(cot_g[...], wo[cols, :]).astype(BF)
 
-    lax.fori_loop(0, 3, attend_back, 0)
-    exchange(peer_a, me_a, m0, m1, 8, False)
-    permute(perm_swap, m1, m2)
-    exchange(peer_b, me_b, m2, m3, 9, True)
-    lax.fori_loop(3, 6, attend_back, 0)
+    lax.fori_loop(0, 6, attend_back, 0)
 
     for half in range(2):
         for n in range(3 * half, 3 * half + 3):
             cols = slice(n * 128, (n + 1) * 128)
             work[:, cols] = nt(gqkv[...], wqkv[cols, :]).astype(BF)
         permute_out(perm_arr, work, g0, half)
-        exchange(peer_a, me_a, g0.at[half], g1.at[half], 10 + half, True)
+        exchange(*second_peer[half], g0.at[half], g1.at[half], 10 + half, True)
+
+    exchange(peer_a, me_a, m0, m1, 8, False)
+    permute(perm_swap, m1, m2)
+    exchange(peer_b, me_b, m2, m3, 9, True)
 
     for d in range(1, 4):
         gp_y(d, False)
@@ -407,9 +416,9 @@
     core.start()
 
     for half in range(2):
-        exchange(peer_a, me_a, g0.at[half], g1.at[half], 10 + half, False)
+        exchange(*second_peer[half], g0.at[half], g1.at[half], 10 + half, False)
         permute_mid(g1, g2, half)
-        exchange(peer_b, me_b, g2.at[half], g3.at[half], 12 + half, True)
+        exchange(*first_peer[half], g2.at[half], g3.at[half], 12 + half, True)
 
     core.wait()
     for k in range(4):
@@ -419,12 +428,12 @@
     gp4[zl] = gp3[zl]
 
     exchange(peer_b, me_b, m2, m3, 9, False)
-    permute(perm_home, m3, work2)
+    permute(perm_home.at[0], m3, work2)
     for l in range(8):
         block_out[l] = (hid[l].astype(F32) + work2[l * 32 : (l + 1) * 32, :].astype(F32)).astype(BF)
 
     for half in range(2):
-        exchange(peer_b, me_b, g2.at[half], g3.at[half], 12 + half, False)
+        exchange(*first_peer[half], g2.at[half], g3.at[half], 12 + half, False)
         permute_in(perm_home, g3, work, half)
     acc[...] = jnp.zeros_like(acc)
 
@@ -441,8 +450,10 @@
         return carry
 
     lax.fori_loop(0, 8, norm_back, 0)
-    fill_edges(normed_w, edges_g)
-    halos = halo_copies(normed_w, edges_g, rows_in_g, cols_in_g, halo_gs, halo_gr)
+    fill_edges(normed_w, edges_g, corners_g)
+    halos = halo_copies(
+        normed_w, edges_g, corners_g, rows_in_g, cols_in_g, corner_in_g, halo_gs, halo_gr
+    )
     for copy in halos:
         copy.start()
 
@@ -480,6 +491,10 @@
 
     sums(peer_a, me_a, s0, s1, 0, False, True)
 
+    sums(peer_a, me_a, s0, s1, 0, False, False)
+    s2[...] = jnp.sum(s1[...], axis=0)
+    sums(peer_b, me_b, s2, s3, 1, True, True)
+
     for d in range(1, 4):
         gp_z(d, False)
     total = gp4[0].astype(F32)
@@ -492,22 +507,19 @@
         gp_l(d, True)
     gp7[a] = gp6[a]
 
-    for copy in halos:
-        copy.wait()
-    fill_shifted(normed_w, rows_in_g, cols_in_g)
-
-    def grad_row(l, carry):
-        grad_fields[l] = conv_row(l, True).astype(BF)
-        return carry
-
-    sums(peer_a, me_a, s0, s1, 0, False, False)
-    s2[...] = jnp.sum(s1[...], axis=0)
-    sums(peer_b, me_b, s2, s3, 1, True, True)
-    lax.fori_loop(0, 6, grad_row, 0)
     sums(peer_b, me_b, s2, s3, 1, True, False)
     s4[...] = jnp.sum(s3[...], axis=0) * TOTAL_SCALE
     sums(peer_a, me_a, s4, s5, 2, True, True)
-    lax.fori_loop(6, 8, grad_row, 0)
+
+    for copy in halos:
+        copy.wait()
+    fill_shifted(normed_w, rows_in_g, cols_in_g, corner_in_g)
+
+    def grad_row(l, carry):
+        grad_fields[l] = conv_row(l, True).astype(BF)
+        return carry
+
+    lax.fori_loop(0, 8, grad_row, 0)
 
     for d in range(1, 8):
         gp_l(d, False)
@@ -534,14 +546,18 @@
         return pltpu.VMEM(shape, dtype)
 
     scratch = (
-        [vmem((D, 3 * D), BF), vmem((D, D), BF), vmem((24, 64, 64), F32), vmem((6, 64, 256), F32), dma((3,))]
+        [vmem((8, 32, D), BF), vmem((8, 32, D), BF), vmem((3, 3, D), F32), vmem((D,), F32), vmem((1, 256), jnp.int32)]
+        + [vmem((D, 3 * D), BF), vmem((D, D), BF), vmem((24, 64, 64), F32), vmem((6, 64, 256), F32), dma((8,))]
+        + [vmem((4, 1, D), BF)] * 4
         + [vmem((2, 8, D), BF), vmem((2, 8, D), BF)]
-        + [vmem((2, 32, D), BF), vmem((6, 8, D), BF)] * 2
+        + [vmem((2, 32, D), BF), vmem((2, 8, D), BF)] * 2
         + [dma((8,))] * 4
         + [vmem((3, 10, 32, D), F32), vmem((8, 32, D), BF), vmem((8, 32, D), F32), vmem((8, 32, 1), F32)]
         + [vmem((256, D), BF)] * 2
         + [vmem((8, 32, D), BF)]
-        + [vmem((256, 256), BF)] * 5
+        + [vmem((2, 256, 256), BF)] * 2
+        + [vmem((256, 256), BF)]
+        + [vmem((2, 256, 256), BF)] * 2
         + [vmem((2, 16, 16, D // 2), BF)] * 12
         + [vmem((16, 16, D), BF)] * 4
         + [dma((14, 16)), dma((14, 16))]
@@ -564,7 +580,7 @@
     out = pl.pallas_call(
         kernel,
         out_shape=results,
-        in_specs=[vm] * 5 + [hbm] * 3,
+        in_specs=[hbm] * 8,
         out_specs=(vm,) * 5,
         scratch_shapes=scratch,
         name="section",

time: 119 us -> 110 us (0.924)
  Pallas kernels: 119 us -> 109 us
    pallas_call x1, Pallas kernels: 116 us -> 107 us  [body(): pl.pallas_call(kernel, out_shape=results, in_specs=[hbm] * 8, out_specs=(...]
where the time goes in v3:
time: 110 us
  Pallas kernels  109 us (99%)
    pallas_call x1, Pallas kernels, body(): pl.pallas_call(kernel, out_shape=results, in_specs=[hbm] * 8, out_specs=(...  107 us

profile of v3, /device:TPU:1, one launch (start us, length us, event | category | flops | bytes accessed | tf_op | source)
XLA Modules:
  0.0 110.1 jit_solution(15489446747595660991)
XLA Ops:
  0.6 107.4 %section.1 = (bf16[8,32,768]{2,1,0:T(8,128)(2,1)}, bf16[8,32,768]{2,1,0:T(8,128)(2,1)}, f32[24,96]{1,0:T(8,128)}, f32[3,3,768]{2,1,0:T(4,128)}, f32[768]{0:T(1024)}) custom-call(bf16[8,32,768]{2,1,0:T(8,128)(2,1)} %fields_hbm.1, bf16[8,32,768]{2,1,0:T(8,128)(2,1)} %cot_hbm.1, f32[3,3,768]{2,1,0:T(4,128)} %taps_hbm.1, f32[768]{0:T(1024)} %gain_hbm.1, ...), custom_call_target="tpu_custom_call" | custom-call | tf_op jit(solution)/shard_map/section/pallas_call | solution.py:580
  108.1 2.1 %results.1 = (bf16[8,32,768]{2,1,0:T(8,128)(2,1)}, bf16[8,32,768]{2,1,0:T(8,128)(2,1)}, f32[24,96]{1,0:T(8,128)}, f32[3,3,768]{2,1,0:T(4,128)}, f32[768]{0:T(1024)}) custom-call(bf16[8,32,768]{2,1,0:T(8,128)(2,1)} %get-tuple-element.15.refs_0_, bf16[8,32,768]{2,1,0:T(8,128)(2,1)} %get-tuple-element.16.refs_1_, f32[24,96]{1,0:T(8,128)} %get-tuple-element.17.refs_2_, ...), custom_call_target="tpu_custom_call" | custom-call | tf_op jit(solution)/shard_map/results/pallas_call | solution.py:594

commit v4 on v3

--- a/solution.py
+++ b/solution.py
@@ -67,7 +67,7 @@
     perm_out, perm_home, perm_swap, perm_pos, perm_arr,
     c0, c1, c2, c3, n0, n1, n2, n3, g0, g1, g2, g3, m0, m1, m2, m3, a2a_s, a2a_r,
     probs, cot_g, nrm_g, qkv, grad_att, att, gqkv,
-    gp0, gp1, gp2, gp3, gp4, gp5, gp6, gp7, gpy_s, gpy_r, gpz_s, gpz_r, gpc_s, gpc_r, gpl_s, gpl_r,
+    gp0, gp1, gp2, gp3, gp4, gp5, gp6, gp7, gp_s, gp_r,
     acc, s0, s1, s2, s3, s4, s5, sum_s, sum_r,
 ):
     a = lax.axis_index("lat")
@@ -131,22 +131,26 @@
         corner[2] = left[7:8].astype(BF)
         corner[3] = right[7:8].astype(BF)
 
-    def halo_copies(source, edge, corner, rows, cols, corner_to, ss, rs):
-        out = []
+    def arrived(ref, sem):
+        pltpu.make_async_copy(ref, ref, sem).wait()
+
+    def halo_start(source, edge, corner, rows, cols, corner_to, ss, rs):
         routes = [
-            (source.at[0], rows.at[1]), (source.at[7], rows.at[0]),
-            (edge.at[0], cols.at[1]), (edge.at[1], cols.at[0]),
-            (corner.at[0], corner_to.at[3]), (corner.at[1], corner_to.at[2]),
-            (corner.at[2], corner_to.at[1]), (corner.at[3], corner_to.at[0]),
+            (source.at[0], rows.at[1], 0), (source.at[7], rows.at[0], 0),
+            (edge.at[0], cols.at[1], 1), (edge.at[1], cols.at[0], 1),
+            (corner.at[0], corner_to.at[3], 2), (corner.at[1], corner_to.at[2], 2),
+            (corner.at[2], corner_to.at[1], 2), (corner.at[3], corner_to.at[0], 2),
         ]
-        for m, (src, dst) in enumerate(routes):
-            out.append(
-                pltpu.make_async_remote_copy(
-                    src_ref=src, dst_ref=dst, send_sem=ss.at[m], recv_sem=rs.at[m],
-                    device_id=neighbour(*offsets[m]), device_id_type=MESH,
-                )
-            )
-        return out
+        for m, (src, dst, kind) in enumerate(routes):
+            pltpu.make_async_remote_copy(
+                src_ref=src, dst_ref=dst, send_sem=ss.at[kind], recv_sem=rs.at[kind],
+                device_id=neighbour(*offsets[m]), device_id_type=MESH,
+            ).start()
+
+    def halo_wait(rows, cols, corner_to, ss, rs):
+        for kind, ref in enumerate((rows, cols, corner_to)):
+            arrived(ref, ss.at[kind])
+            arrived(ref, rs.at[kind])
 
     top_mask = (a > 0).astype(F32)
     bottom_mask = (a < 7).astype(F32)
@@ -170,22 +174,22 @@
             shifted[2, r] = jnp.where(row32 == 31, ri, pltpu.roll(f, 31, 0))
 
     def exchange(peer, me, src, dst, slot, sends):
+        if not sends:
+            arrived(src.at[pl.ds(0, 15)], a2a_s.at[slot])
+            arrived(dst.at[pl.ds(0, 15)], a2a_r.at[slot])
+            return
+
         def step(d, carry):
             k = rem(me + d, 16)
-            copy = pltpu.make_async_remote_copy(
-                src_ref=src.at[k], dst_ref=dst.at[me] if sends else dst.at[k],
-                send_sem=a2a_s.at[slot, d], recv_sem=a2a_r.at[slot, me if sends else k],
+            pltpu.make_async_remote_copy(
+                src_ref=src.at[k], dst_ref=dst.at[me],
+                send_sem=a2a_s.at[slot], recv_sem=a2a_r.at[slot],
                 device_id=peer(k), device_id_type=MESH,
-            )
-            if sends:
-                copy.start()
-            else:
-                copy.wait()
+            ).start()
             return carry
 
         lax.fori_loop(1, 16, step, 0)
-        if sends:
-            dst[me] = src[me]
+        dst[me] = src[me]
 
     def permute(perm, src, dst):
         for n in range(3):
@@ -208,9 +212,7 @@
     loads["fields"].wait()
     fill_edges(fields, edges, corners)
     pl.semaphore_wait(bar, 41)
-    halos = halo_copies(fields, edges, corners, rows_in, cols_in, corner_in, halo_s, halo_r)
-    for copy in halos:
-        copy.start()
+    halo_start(fields, edges, corners, rows_in, cols_in, corner_in, halo_s, halo_r)
 
     loads["pat"].wait()
     pat_hot = one_hot(iota2(0) == pat[...])
@@ -233,8 +235,7 @@
     for q in range(6):
         bias_t[q] = jnp.transpose(bias[4 * q : 4 * q + 4].reshape(256, 64))
 
-    for copy in halos:
-        copy.wait()
+    halo_wait(rows_in, cols_in, corner_in, halo_s, halo_r)
     exchange(*first_peer[1], c0.at[1], c1.at[1], 5, True)
     fill_shifted(fields, rows_in, cols_in, corner_in)
     loads["taps"].wait()
@@ -282,12 +283,9 @@
         permute_in(perm_pos, n3, nrm_g, h)
     loads["wqkv"].wait()
 
-    def project(n, carry):
-        cols = pl.ds(pl.multiple_of(n * 256, 256), 256)
+    for n in range(6):
+        cols = slice(n * 384, (n + 1) * 384)
         qkv[:, cols] = nn(nrm_g[...], wqkv[:, cols]).astype(BF)
-        return carry
-
-    lax.fori_loop(0, 9, project, 0)
 
     lane_head = lax.broadcasted_iota(jnp.int32, (64, 128), 1) >> 5
 
@@ -352,35 +350,33 @@
 
     lax.fori_loop(0, 2, outer, 0)
 
-    def gp_y(d, sends):
+    def gp_y(d):
         k = rem(y + d, 4)
-        copy = pltpu.make_async_remote_copy(
-            src_ref=gp0.at[:, k], dst_ref=gp1.at[y] if sends else gp1.at[k],
-            send_sem=gpy_s.at[d], recv_sem=gpy_r.at[y if sends else k],
+        pltpu.make_async_remote_copy(
+            src_ref=gp0.at[:, k], dst_ref=gp1.at[y], send_sem=gp_s.at[0], recv_sem=gp_r.at[0],
             device_id=device(x, k, z, c), device_id_type=MESH,
-        )
-        copy.start() if sends else copy.wait()
-
-    def gp_z(d, sends):
+        ).start()
+
+    def gp_z(d):
         k = rem(zl + d, 4)
-        copy = pltpu.make_async_remote_copy(
-            src_ref=gp3.at[k], dst_ref=gp4.at[zl] if sends else gp4.at[k],
-            send_sem=gpz_s.at[d], recv_sem=gpz_r.at[zl if sends else k],
+        pltpu.make_async_remote_copy(
+            src_ref=gp3.at[k], dst_ref=gp4.at[zl], send_sem=gp_s.at[2], recv_sem=gp_r.at[2],
             device_id=device(x, y, zh * 4 + k, c), device_id_type=MESH,
-        )
-        copy.start() if sends else copy.wait()
-
-    def gp_l(d, sends):
+        ).start()
+
+    def gp_l(d):
         k = rem(a + d, 8)
-        copy = pltpu.make_async_remote_copy(
-            src_ref=gp6.at[k], dst_ref=gp7.at[a] if sends else gp7.at[k],
-            send_sem=gpl_s.at[d], recv_sem=gpl_r.at[a if sends else k],
+        pltpu.make_async_remote_copy(
+            src_ref=gp6.at[k], dst_ref=gp7.at[a], send_sem=gp_s.at[3], recv_sem=gp_r.at[3],
             device_id=(k, b), device_id_type=MESH,
-        )
-        copy.start() if sends else copy.wait()
+        ).start()
+
+    def gp_arrived(ref, n, stage):
+        arrived(ref.at[pl.ds(0, n)], gp_s.at[stage])
+        arrived(ref.at[pl.ds(0, n)], gp_r.at[stage])
 
     for d in range(1, 4):
-        gp_y(d, True)
+        gp_y(d)
     for k in range(4):
         gp1[y, k] = gp0[k, y]
 
@@ -391,9 +387,8 @@
     lax.fori_loop(0, 6, attend_back, 0)
 
     for half in range(2):
-        for n in range(3 * half, 3 * half + 3):
-            cols = slice(n * 128, (n + 1) * 128)
-            work[:, cols] = nt(gqkv[...], wqkv[cols, :]).astype(BF)
+        cols = slice(half * 384, (half + 1) * 384)
+        work[:, cols] = nt(gqkv[...], wqkv[cols, :]).astype(BF)
         permute_out(perm_arr, work, g0, half)
         exchange(*second_peer[half], g0.at[half], g1.at[half], 10 + half, True)
 
@@ -401,8 +396,7 @@
     permute(perm_swap, m1, m2)
     exchange(peer_b, me_b, m2, m3, 9, True)
 
-    for d in range(1, 4):
-        gp_y(d, False)
+    gp_arrived(gp1, 3, 0)
     for k in range(4):
         total = gp1[0, k].astype(F32)
         for i in range(1, 4):
@@ -410,7 +404,7 @@
         gp2[0, k] = total[0:24]
         gp2[1, k] = total[24:48]
     core = pltpu.make_async_remote_copy(
-        src_ref=gp2.at[1 - c], dst_ref=gp5, send_sem=gpc_s, recv_sem=gpc_r,
+        src_ref=gp2.at[1 - c], dst_ref=gp5, send_sem=gp_s.at[1], recv_sem=gp_r.at[1],
         device_id=device(x, y, z, 1 - c), device_id_type=MESH,
     )
     core.start()
@@ -424,7 +418,7 @@
     for k in range(4):
         gp3[k] = (gp2[c, k] + gp5[k]).astype(BF)
     for d in range(1, 4):
-        gp_z(d, True)
+        gp_z(d)
     gp4[zl] = gp3[zl]
 
     exchange(peer_b, me_b, m2, m3, 9, False)
@@ -451,11 +445,7 @@
 
     lax.fori_loop(0, 8, norm_back, 0)
     fill_edges(normed_w, edges_g, corners_g)
-    halos = halo_copies(
-        normed_w, edges_g, corners_g, rows_in_g, cols_in_g, corner_in_g, halo_gs, halo_gr
-    )
-    for copy in halos:
-        copy.start()
+    halo_start(normed_w, edges_g, corners_g, rows_in_g, cols_in_g, corner_in_g, halo_gs, halo_gr)
 
     def tap_sums(l, carry):
         gh = normed_w[l].astype(F32)
@@ -472,22 +462,22 @@
             s0[k] = jnp.zeros((1, D), F32)
 
     def sums(peer, me, src, dst, slot, whole_src, sends):
+        if not sends:
+            arrived(dst.at[pl.ds(0, 15)], sum_s.at[slot])
+            arrived(dst.at[pl.ds(0, 15)], sum_r.at[slot])
+            return
+
         def step(d, carry):
             k = rem(me + d, 16)
-            copy = pltpu.make_async_remote_copy(
-                src_ref=src if whole_src else src.at[k], dst_ref=dst.at[me] if sends else dst.at[k],
-                send_sem=sum_s.at[slot, d], recv_sem=sum_r.at[slot, me if sends else k],
+            pltpu.make_async_remote_copy(
+                src_ref=src if whole_src else src.at[k], dst_ref=dst.at[me],
+                send_sem=sum_s.at[slot], recv_sem=sum_r.at[slot],
                 device_id=peer(k), device_id_type=MESH,
-            )
-            if sends:
-                copy.start()
-            else:
-                copy.wait()
+            ).start()
             return carry
 
         lax.fori_loop(1, 16, step, 0)
-        if sends:
-            dst[me] = src[...] if whole_src else src[me]
+        dst[me] = src[...] if whole_src else src[me]
 
     sums(peer_a, me_a, s0, s1, 0, False, True)
 
@@ -495,8 +485,7 @@
     s2[...] = jnp.sum(s1[...], axis=0)
     sums(peer_b, me_b, s2, s3, 1, True, True)
 
-    for d in range(1, 4):
-        gp_z(d, False)
+    gp_arrived(gp4, 3, 2)
     total = gp4[0].astype(F32)
     for i in range(1, 4):
         total = total + gp4[i].astype(F32)
@@ -504,15 +493,14 @@
         gp6[i, :, 0:96] = total[:, i * 96 : (i + 1) * 96]
         gp6[i, :, 96:128] = jnp.zeros((24, 32), F32)
     for d in range(1, 8):
-        gp_l(d, True)
+        gp_l(d)
     gp7[a] = gp6[a]
 
     sums(peer_b, me_b, s2, s3, 1, True, False)
     s4[...] = jnp.sum(s3[...], axis=0) * TOTAL_SCALE
     sums(peer_a, me_a, s4, s5, 2, True, True)
 
-    for copy in halos:
-        copy.wait()
+    halo_wait(rows_in_g, cols_in_g, corner_in_g, halo_gs, halo_gr)
     fill_shifted(normed_w, rows_in_g, cols_in_g, corner_in_g)
 
     def grad_row(l, carry):
@@ -521,8 +509,7 @@
 
     lax.fori_loop(0, 8, grad_row, 0)
 
-    for d in range(1, 8):
-        gp_l(d, False)
+    gp_arrived(gp7, 7, 3)
     gp_out[...] = (jnp.sum(gp7[...], axis=0) * TOTAL_SCALE)[:, 0:96]
     sums(peer_a, me_a, s4, s5, 2, True, False)
     for k in range(9):
@@ -551,7 +538,7 @@
         + [vmem((4, 1, D), BF)] * 4
         + [vmem((2, 8, D), BF), vmem((2, 8, D), BF)]
         + [vmem((2, 32, D), BF), vmem((2, 8, D), BF)] * 2
-        + [dma((8,))] * 4
+        + [dma((3,))] * 4
         + [vmem((3, 10, 32, D), F32), vmem((8, 32, D), BF), vmem((8, 32, D), F32), vmem((8, 32, 1), F32)]
         + [vmem((256, D), BF)] * 2
         + [vmem((8, 32, D), BF)]
@@ -560,15 +547,15 @@
         + [vmem((2, 256, 256), BF)] * 2
         + [vmem((2, 16, 16, D // 2), BF)] * 12
         + [vmem((16, 16, D), BF)] * 4
-        + [dma((14, 16)), dma((14, 16))]
+        + [dma((14,)), dma((14,))]
         + [vmem((6, 4, 64, 256), F32)]
         + [vmem((256, D), BF), vmem((256, D), BF), vmem((256, 3 * D), BF), vmem((256, D), BF), vmem((256, D), BF), vmem((256, 3 * D), BF)]
         + [vmem((4, 4, 48, D), BF), vmem((4, 4, 48, D), BF), vmem((2, 4, 24, D), F32)]
         + [vmem((4, 24, D), BF), vmem((4, 24, D), BF), vmem((4, 24, D), F32)]
         + [vmem((8, 24, 128), F32), vmem((8, 24, 128), F32)]
-        + [dma((4,)), dma((4,)), dma((4,)), dma((4,)), dma(()), dma(()), dma((8,)), dma((8,))]
+        + [dma((4,)), dma((4,))]
         + [vmem((10, 8, D), F32), vmem((16, 1, D), F32), vmem((16, 1, D), F32), vmem((1, D), F32), vmem((16, 1, D), F32), vmem((1, D), F32), vmem((16, 1, D), F32)]
-        + [dma((3, 16)), dma((3, 16))]
+        + [dma((3,)), dma((3,))]
     )
     results = (
         jax.ShapeDtypeStruct((8, 32, D), BF),

time: 110 us -> 102 us (0.927)
  Pallas kernels: 109 us -> 101 us
    pallas_call x1, Pallas kernels: 107 us -> 99.2 us  [body(): pl.pallas_call(kernel, out_shape=results, in_specs=[hbm] * 8, out_specs=(...]
where the time goes in v4:
time: 102 us
  Pallas kernels  101 us (99%)
    pallas_call x1, Pallas kernels, body(): pl.pallas_call(kernel, out_shape=results, in_specs=[hbm] * 8, out_specs=(...  99.2 us
    pallas_call x1, Pallas kernels, body(): pl.pallas_call(hand_over, out_shape=results, in_specs=[vm] * 5, out_specs...  2.06 us

profile of v4, /device:TPU:1, one launch (start us, length us, event | category | flops | bytes accessed | tf_op | source)
XLA Modules:
  0.0 101.9 jit_solution(7039948287661455441)
XLA Ops:
  0.6 99.2 %section.1 = (bf16[8,32,768]{2,1,0:T(8,128)(2,1)}, bf16[8,32,768]{2,1,0:T(8,128)(2,1)}, f32[24,96]{1,0:T(8,128)}, f32[3,3,768]{2,1,0:T(4,128)}, f32[768]{0:T(1024)}) custom-call(bf16[8,32,768]{2,1,0:T(8,128)(2,1)} %fields_hbm.1, bf16[8,32,768]{2,1,0:T(8,128)(2,1)} %cot_hbm.1, f32[3,3,768]{2,1,0:T(4,128)} %taps_hbm.1, f32[768]{0:T(1024)} %gain_hbm.1, ...), custom_call_target="tpu_custom_call" | custom-call | tf_op jit(solution)/shard_map/section/pallas_call | solution.py:567
  99.9 2.1 %results.1 = (bf16[8,32,768]{2,1,0:T(8,128)(2,1)}, bf16[8,32,768]{2,1,0:T(8,128)(2,1)}, f32[24,96]{1,0:T(8,128)}, f32[3,3,768]{2,1,0:T(4,128)}, f32[768]{0:T(1024)}) custom-call(bf16[8,32,768]{2,1,0:T(8,128)(2,1)} %get-tuple-element.15.refs_0_, bf16[8,32,768]{2,1,0:T(8,128)(2,1)} %get-tuple-element.16.refs_1_, f32[24,96]{1,0:T(8,128)} %get-tuple-element.17.refs_2_, ...), custom_call_target="tpu_custom_call" | custom-call | tf_op jit(solution)/shard_map/results/pallas_call | solution.py:581

commit v5 on v4

--- a/solution.py
+++ b/solution.py
@@ -66,7 +66,7 @@
     shifted, hid, xhat, rstd, work, work2, normed_w,
     perm_out, perm_home, perm_swap, perm_pos, perm_arr,
     c0, c1, c2, c3, n0, n1, n2, n3, g0, g1, g2, g3, m0, m1, m2, m3, a2a_s, a2a_r,
-    probs, cot_g, nrm_g, qkv, grad_att, att, gqkv,
+    qkv_part, block_v, grad_v, out_sem, probs, cot_g, nrm_g, qkv, grad_att, att, gqkv,
     gp0, gp1, gp2, gp3, gp4, gp5, gp6, gp7, gp_s, gp_r,
     acc, s0, s1, s2, s3, s4, s5, sum_s, sum_r,
 ):
@@ -134,7 +134,7 @@
     def arrived(ref, sem):
         pltpu.make_async_copy(ref, ref, sem).wait()
 
-    def halo_start(source, edge, corner, rows, cols, corner_to, ss, rs):
+    def halo_start(kinds, source, edge, corner, rows, cols, corner_to, ss, rs):
         routes = [
             (source.at[0], rows.at[1], 0), (source.at[7], rows.at[0], 0),
             (edge.at[0], cols.at[1], 1), (edge.at[1], cols.at[0], 1),
@@ -142,6 +142,8 @@
             (corner.at[2], corner_to.at[1], 2), (corner.at[3], corner_to.at[0], 2),
         ]
         for m, (src, dst, kind) in enumerate(routes):
+            if kind not in kinds:
+                continue
             pltpu.make_async_remote_copy(
                 src_ref=src, dst_ref=dst, send_sem=ss.at[kind], recv_sem=rs.at[kind],
                 device_id=neighbour(*offsets[m]), device_id_type=MESH,
@@ -155,23 +157,26 @@
     top_mask = (a > 0).astype(F32)
     bottom_mask = (a < 7).astype(F32)
 
-    def fill_shifted(source, rows, cols, corner):
-        for r in range(10):
-            if r == 0:
-                f = rows[0].astype(F32) * top_mask
-                le = corner[0].astype(F32) * top_mask
-                ri = corner[1].astype(F32) * top_mask
-            elif r == 9:
-                f = rows[1].astype(F32) * bottom_mask
-                le = corner[2].astype(F32) * bottom_mask
-                ri = corner[3].astype(F32) * bottom_mask
-            else:
-                f = source[r - 1].astype(F32)
-                le = cols[0].astype(F32)[r - 1 : r, :]
-                ri = cols[1].astype(F32)[r - 1 : r, :]
+    def fill_inside(source):
+        for r in range(1, 9):
+            f = source[r - 1].astype(F32)
+            shifted[0, r] = pltpu.roll(f, 1, 0)
+            shifted[1, r] = f
+            shifted[2, r] = pltpu.roll(f, 31, 0)
+
+    def fill_rim(rows, cols, corner):
+        for r, n, mask in ((0, 0, top_mask), (9, 1, bottom_mask)):
+            f = rows[n].astype(F32) * mask
+            le = corner[2 * n].astype(F32) * mask
+            ri = corner[2 * n + 1].astype(F32) * mask
             shifted[0, r] = jnp.where(row32 == 0, le, pltpu.roll(f, 1, 0))
             shifted[1, r] = f
             shifted[2, r] = jnp.where(row32 == 31, ri, pltpu.roll(f, 31, 0))
+        le = cols[0].astype(F32)
+        ri = cols[1].astype(F32)
+        for r in range(1, 9):
+            shifted[0, r, 0:1, :] = le[r - 1 : r, :]
+            shifted[2, r, 31:32, :] = ri[r - 1 : r, :]
 
     def exchange(peer, me, src, dst, slot, sends):
         if not sends:
@@ -188,7 +193,7 @@
             ).start()
             return carry
 
-        lax.fori_loop(1, 16, step, 0)
+        lax.fori_loop(1, 16, step, 0, unroll=15)
         dst[me] = src[me]
 
     def permute(perm, src, dst):
@@ -212,7 +217,7 @@
     loads["fields"].wait()
     fill_edges(fields, edges, corners)
     pl.semaphore_wait(bar, 41)
-    halo_start(fields, edges, corners, rows_in, cols_in, corner_in, halo_s, halo_r)
+    halo_start((0, 1, 2), fields, edges, corners, rows_in, cols_in, corner_in, halo_s, halo_r)
 
     loads["pat"].wait()
     pat_hot = one_hot(iota2(0) == pat[...])
@@ -235,9 +240,10 @@
     for q in range(6):
         bias_t[q] = jnp.transpose(bias[4 * q : 4 * q + 4].reshape(256, 64))
 
+    fill_inside(fields)
     halo_wait(rows_in, cols_in, corner_in, halo_s, halo_r)
     exchange(*first_peer[1], c0.at[1], c1.at[1], 5, True)
-    fill_shifted(fields, rows_in, cols_in, corner_in)
+    fill_rim(rows_in, cols_in, corner_in)
     loads["taps"].wait()
     loads["gain"].wait()
     gain_row = gain[...].reshape(1, D)
@@ -264,7 +270,7 @@
         normed_w[l] = (xh * gain_row).astype(BF)
         return carry
 
-    lax.fori_loop(0, 8, norm_row, 0)
+    lax.fori_loop(0, 8, norm_row, 0, unroll=2)
     for h in range(2):
         permute_out(perm_out, normed_w, n0, h)
         exchange(*first_peer[h], n0.at[h], n1.at[h], h, True)
@@ -278,14 +284,17 @@
     for h in range(2):
         exchange(*second_peer[h], c2.at[h], c3.at[h], 6 + h, True)
 
-    for h in (1, 0):
-        exchange(*second_peer[h], n2.at[h], n3.at[h], 2 + h, False)
-        permute_in(perm_pos, n3, nrm_g, h)
+    exchange(*second_peer[1], n2.at[1], n3.at[1], 3, False)
+    permute_in(perm_pos, n3, nrm_g, 1)
     loads["wqkv"].wait()
-
     for n in range(6):
         cols = slice(n * 384, (n + 1) * 384)
-        qkv[:, cols] = nn(nrm_g[...], wqkv[:, cols]).astype(BF)
+        qkv_part[:, cols] = nn(nrm_g[:, 384:], wqkv[384:, cols])
+    exchange(*second_peer[0], n2.at[0], n3.at[0], 2, False)
+    permute_in(perm_pos, n3, nrm_g, 0)
+    for n in range(6):
+        cols = slice(n * 384, (n + 1) * 384)
+        qkv[:, cols] = (nn(nrm_g[:, :384], wqkv[:384, cols]) + qkv_part[:, cols]).astype(BF)
 
     lane_head = lax.broadcasted_iota(jnp.int32, (64, 128), 1) >> 5
 
@@ -396,6 +405,11 @@
     permute(perm_swap, m1, m2)
     exchange(peer_b, me_b, m2, m3, 9, True)
 
+    for half in range(2):
+        exchange(*second_peer[half], g0.at[half], g1.at[half], 10 + half, False)
+        permute_mid(g1, g2, half)
+        exchange(*first_peer[half], g2.at[half], g3.at[half], 12 + half, True)
+
     gp_arrived(gp1, 3, 0)
     for k in range(4):
         total = gp1[0, k].astype(F32)
@@ -409,10 +423,12 @@
     )
     core.start()
 
-    for half in range(2):
-        exchange(*second_peer[half], g0.at[half], g1.at[half], 10 + half, False)
-        permute_mid(g1, g2, half)
-        exchange(*first_peer[half], g2.at[half], g3.at[half], 12 + half, True)
+    exchange(peer_b, me_b, m2, m3, 9, False)
+    permute(perm_home.at[0], m3, work2)
+    for l in range(8):
+        block_v[l] = (hid[l].astype(F32) + work2[l * 32 : (l + 1) * 32, :].astype(F32)).astype(BF)
+    block_copy = pltpu.make_async_copy(block_v, block_out, out_sem.at[8])
+    block_copy.start()
 
     core.wait()
     for k in range(4):
@@ -421,18 +437,14 @@
         gp_z(d)
     gp4[zl] = gp3[zl]
 
-    exchange(peer_b, me_b, m2, m3, 9, False)
-    permute(perm_home.at[0], m3, work2)
-    for l in range(8):
-        block_out[l] = (hid[l].astype(F32) + work2[l * 32 : (l + 1) * 32, :].astype(F32)).astype(BF)
-
     for half in range(2):
         exchange(*first_peer[half], g2.at[half], g3.at[half], 12 + half, False)
         permute_in(perm_home, g3, work, half)
     acc[...] = jnp.zeros_like(acc)
 
     def norm_back(l, carry):
-        ng = work[pl.ds(pl.multiple_of(l * 32, 32), 32), :].astype(F32)
+        at = l * 32 if isinstance(l, int) else pl.multiple_of(l * 32, 32)
+        ng = work[pl.ds(at, 32), :].astype(F32)
         xh = xhat[l]
         prod = ng * xh
         acc[9] += jnp.sum(prod.reshape(4, 8, D), axis=0)
@@ -443,9 +455,13 @@
         normed_w[l] = gh.astype(BF)
         return carry
 
-    lax.fori_loop(0, 8, norm_back, 0)
+    halo_g = (normed_w, edges_g, corners_g, rows_in_g, cols_in_g, corner_in_g, halo_gs, halo_gr)
+    norm_back(0, 0)
+    norm_back(7, 0)
+    halo_start((0,), *halo_g)
+    lax.fori_loop(1, 7, norm_back, 0, unroll=2)
     fill_edges(normed_w, edges_g, corners_g)
-    halo_start(normed_w, edges_g, corners_g, rows_in_g, cols_in_g, corner_in_g, halo_gs, halo_gr)
+    halo_start((1, 2), *halo_g)
 
     def tap_sums(l, carry):
         gh = normed_w[l].astype(F32)
@@ -454,7 +470,7 @@
                 acc[3 * i + j] += jnp.sum((shifted[j, l + i] * gh).reshape(4, 8, D), axis=0)
         return carry
 
-    lax.fori_loop(0, 8, tap_sums, 0)
+    lax.fori_loop(0, 8, tap_sums, 0, unroll=2)
     for k in range(16):
         if k < 10:
             s0[k] = jnp.sum(acc[k], axis=0, keepdims=True)
@@ -476,14 +492,15 @@
             ).start()
             return carry
 
-        lax.fori_loop(1, 16, step, 0)
+        lax.fori_loop(1, 16, step, 0, unroll=15)
         dst[me] = src[...] if whole_src else src[me]
 
-    sums(peer_a, me_a, s0, s1, 0, False, True)
-
-    sums(peer_a, me_a, s0, s1, 0, False, False)
+    sums(peer_b, me_b, s0, s1, 0, False, True)
+    fill_inside(normed_w)
+
+    sums(peer_b, me_b, s0, s1, 0, False, False)
     s2[...] = jnp.sum(s1[...], axis=0)
-    sums(peer_b, me_b, s2, s3, 1, True, True)
+    sums(peer_a, me_a, s2, s3, 1, True, True)
 
     gp_arrived(gp4, 3, 2)
     total = gp4[0].astype(F32)
@@ -496,30 +513,45 @@
         gp_l(d)
     gp7[a] = gp6[a]
 
-    sums(peer_b, me_b, s2, s3, 1, True, False)
+    sums(peer_a, me_a, s2, s3, 1, True, False)
     s4[...] = jnp.sum(s3[...], axis=0) * TOTAL_SCALE
-    sums(peer_a, me_a, s4, s5, 2, True, True)
+    sums(peer_b, me_b, s4, s5, 2, True, True)
 
     halo_wait(rows_in_g, cols_in_g, corner_in_g, halo_gs, halo_gr)
-    fill_shifted(normed_w, rows_in_g, cols_in_g, corner_in_g)
+    fill_rim(rows_in_g, cols_in_g, corner_in_g)
 
     def grad_row(l, carry):
-        grad_fields[l] = conv_row(l, True).astype(BF)
-        return carry
-
-    lax.fori_loop(0, 8, grad_row, 0)
+        grad_v[l] = conv_row(l, True).astype(BF)
+        pltpu.make_async_copy(grad_v.at[l], grad_fields.at[l], out_sem.at[l]).start()
+        return carry
+
+    lax.fori_loop(0, 8, grad_row, 0, unroll=2)
 
     gp_arrived(gp7, 7, 3)
     gp_out[...] = (jnp.sum(gp7[...], axis=0) * TOTAL_SCALE)[:, 0:96]
-    sums(peer_a, me_a, s4, s5, 2, True, False)
+    sums(peer_b, me_b, s4, s5, 2, True, False)
     for k in range(9):
         taps_out[k // 3, k % 3 : k % 3 + 1, :] = s5[k]
     gain_out[...] = s5[9].reshape(D)
+    block_copy.wait()
+    for l in range(8):
+        pltpu.make_async_copy(grad_v.at[l], grad_fields.at[l], out_sem.at[l]).wait()
 
 
 def hand_over(*refs):
+    sems = refs[10]
+    copies = []
     for k in range(5):
-        refs[5 + k][...] = refs[k][...]
+        if k < 2:
+            for l in range(8):
+                copies.append((refs[k].at[l], refs[5 + k].at[l]))
+        else:
+            copies.append((refs[k], refs[5 + k]))
+    copies = [pltpu.make_async_copy(src, dst, sems.at[i]) for i, (src, dst) in enumerate(copies)]
+    for copy in copies:
+        copy.start()
+    for copy in copies:
+        copy.wait()
 
 
 def body(
@@ -548,6 +580,7 @@
         + [vmem((2, 16, 16, D // 2), BF)] * 12
         + [vmem((16, 16, D), BF)] * 4
         + [dma((14,)), dma((14,))]
+        + [vmem((256, 3 * D), F32), vmem((8, 32, D), BF), vmem((8, 32, D), BF), dma((9,))]
         + [vmem((6, 4, 64, 256), F32)]
         + [vmem((256, D), BF), vmem((256, D), BF), vmem((256, 3 * D), BF), vmem((256, D), BF), vmem((256, D), BF), vmem((256, 3 * D), BF)]
         + [vmem((4, 4, 48, D), BF), vmem((4, 4, 48, D), BF), vmem((2, 4, 24, D), F32)]
@@ -568,7 +601,7 @@
         kernel,
         out_shape=results,
         in_specs=[hbm] * 8,
-        out_specs=(vm,) * 5,
+        out_specs=(hbm,) * 2 + (vm,) * 3,
         scratch_shapes=scratch,
         name="section",
         compiler_params=pltpu.CompilerParams(
@@ -579,7 +612,8 @@
         pattern.reshape(1, 256), qkv_weight, out_weight, score_bias,
     )
     block_out, grad_fields, gp, taps, gain = pl.pallas_call(
-        hand_over, out_shape=results, in_specs=[vm] * 5, out_specs=(vm,) * 5, name="results"
+        hand_over, out_shape=results, in_specs=[hbm] * 5, out_specs=(hbm,) * 5,
+        scratch_shapes=[dma((19,))], name="results",
     )(*out)
     return (block_out, grad_fields, jnp.transpose(gp), taps, gain)
 

time: 102 us -> 124 us (1.22)
  Pallas kernels: 101 us -> 123 us
    pallas_call x1, Pallas kernels: 2.06 us -> 26.7 us  [body(): pl.pallas_call(hand_over, out_shape=results, in_specs=[hbm] * 5, out_spec...]
    pallas_call x1, Pallas kernels: 99.2 us -> 96.1 us  [body(): pl.pallas_call(kernel, out_shape=results, in_specs=[hbm] * 8, out_specs=(...]
where the time goes in v5:
time: 124 us; the launch traced here: 123 us
  Pallas kernels  123 us (99%)
    pallas_call x1, Pallas kernels, body(): pl.pallas_call(kernel, out_shape=results, in_specs=[hbm] * 8, out_specs=(...  96.1 us
    pallas_call x1, Pallas kernels, body(): pl.pallas_call(hand_over, out_shape=results, in_specs=[hbm] * 5, out_spec...  26.7 us

profile of v5, /device:TPU:1, one launch (start us, length us, event | category | flops | bytes accessed | tf_op | source)
XLA Modules:
  0.0 123.4 jit_solution(1015042603495675752)
XLA Ops:
  0.6 96.1 %section.1 = (bf16[8,32,768]{2,1,0:T(8,128)(2,1)}, bf16[8,32,768]{2,1,0:T(8,128)(2,1)}, f32[24,96]{1,0:T(8,128)}, f32[3,3,768]{2,1,0:T(4,128)}, f32[768]{0:T(1024)}) custom-call(bf16[8,32,768]{2,1,0:T(8,128)(2,1)} %fields_hbm.1, bf16[8,32,768]{2,1,0:T(8,128)(2,1)} %cot_hbm.1, f32[3,3,768]{2,1,0:T(4,128)} %taps_hbm.1, f32[768]{0:T(1024)} %gain_hbm.1, ...), custom_call_target="tpu_custom_call" | custom-call | tf_op jit(solution)/shard_map/section/pallas_call | solution.py:600
  96.8 26.7 %results.1 = (bf16[8,32,768]{2,1,0:T(8,128)(2,1)}, bf16[8,32,768]{2,1,0:T(8,128)(2,1)}, f32[24,96]{1,0:T(8,128)}, f32[3,3,768]{2,1,0:T(4,128)}, f32[768]{0:T(1024)}) custom-call(bf16[8,32,768]{2,1,0:T(8,128)(2,1)} %get-tuple-element.15.refs_0_, bf16[8,32,768]{2,1,0:T(8,128)(2,1)} %get-tuple-element.16.refs_1_, f32[24,96]{1,0:T(8,128)} %get-tuple-element.17.refs_2_, ...), custom_call_target="tpu_custom_call" | custom-call | tf_op jit(solution)/shard_map/results/pallas_call | solution.py:614

commit v6 on v5

--- a/solution.py
+++ b/solution.py
@@ -67,7 +67,7 @@
     perm_out, perm_home, perm_swap, perm_pos, perm_arr,
     c0, c1, c2, c3, n0, n1, n2, n3, g0, g1, g2, g3, m0, m1, m2, m3, a2a_s, a2a_r,
     qkv_part, block_v, grad_v, out_sem, probs, cot_g, nrm_g, qkv, grad_att, att, gqkv,
-    gp0, gp1, gp2, gp3, gp4, gp5, gp6, gp7, gp_s, gp_r,
+    gp0, gpx, gpa, gp1, gp3, gp4, gp6, gp7, gp_s, gp_r,
     acc, s0, s1, s2, s3, s4, s5, sum_s, sum_r,
 ):
     a = lax.axis_index("lat")
@@ -353,16 +353,21 @@
 
     def outer(n, carry):
         cols = pl.ds(pl.multiple_of(n * 384, 128), 384)
-        got = tn(cot_g[:, cols], att[...]).astype(BF)
-        gp0[pl.ds(2 * n, 2)] = got.reshape(2, 4, 48, D)
+        got = tn(cot_g[:, cols], att[...])
+        gp0[pl.ds(2 * n, 2)] = got.reshape(2, 4, 2, 24, D).astype(BF)
         return carry
 
     lax.fori_loop(0, 2, outer, 0)
+    core = pltpu.make_async_remote_copy(
+        src_ref=gp0.at[:, :, 1 - c], dst_ref=gpx, send_sem=gp_s.at[1], recv_sem=gp_r.at[1],
+        device_id=device(x, y, z, 1 - c), device_id_type=MESH,
+    )
+    core.start()
 
     def gp_y(d):
         k = rem(y + d, 4)
         pltpu.make_async_remote_copy(
-            src_ref=gp0.at[:, k], dst_ref=gp1.at[y], send_sem=gp_s.at[0], recv_sem=gp_r.at[0],
+            src_ref=gpa.at[:, k], dst_ref=gp1.at[y], send_sem=gp_s.at[0], recv_sem=gp_r.at[0],
             device_id=device(x, k, z, c), device_id_type=MESH,
         ).start()
 
@@ -384,16 +389,19 @@
         arrived(ref.at[pl.ds(0, n)], gp_s.at[stage])
         arrived(ref.at[pl.ds(0, n)], gp_r.at[stage])
 
+    for n in range(3):
+        cols = slice(n * 256, (n + 1) * 256)
+        grad_att[:, cols] = nt(cot_g[...], wo[cols, :]).astype(BF)
+
+    lax.fori_loop(0, 3, attend_back, 0)
+    core.wait()
+    for k in range(4):
+        gpa[k] = (gp0[k, :, c].astype(F32) + gpx[k].astype(F32)).astype(BF)
     for d in range(1, 4):
         gp_y(d)
     for k in range(4):
-        gp1[y, k] = gp0[k, y]
-
-    for n in range(3):
-        cols = slice(n * 256, (n + 1) * 256)
-        grad_att[:, cols] = nt(cot_g[...], wo[cols, :]).astype(BF)
-
-    lax.fori_loop(0, 6, attend_back, 0)
+        gp1[y, k] = gpa[k, y]
+    lax.fori_loop(3, 6, attend_back, 0)
 
     for half in range(2):
         cols = slice(half * 384, (half + 1) * 384)
@@ -415,13 +423,10 @@
         total = gp1[0, k].astype(F32)
         for i in range(1, 4):
             total = total + gp1[i, k].astype(F32)
-        gp2[0, k] = total[0:24]
-        gp2[1, k] = total[24:48]
-    core = pltpu.make_async_remote_copy(
-        src_ref=gp2.at[1 - c], dst_ref=gp5, send_sem=gp_s.at[1], recv_sem=gp_r.at[1],
-        device_id=device(x, y, z, 1 - c), device_id_type=MESH,
-    )
-    core.start()
+        gp3[k] = total.astype(BF)
+    for d in range(1, 4):
+        gp_z(d)
+    gp4[zl] = gp3[zl]
 
     exchange(peer_b, me_b, m2, m3, 9, False)
     permute(perm_home.at[0], m3, work2)
@@ -429,13 +434,6 @@
         block_v[l] = (hid[l].astype(F32) + work2[l * 32 : (l + 1) * 32, :].astype(F32)).astype(BF)
     block_copy = pltpu.make_async_copy(block_v, block_out, out_sem.at[8])
     block_copy.start()
-
-    core.wait()
-    for k in range(4):
-        gp3[k] = (gp2[c, k] + gp5[k]).astype(BF)
-    for d in range(1, 4):
-        gp_z(d)
-    gp4[zl] = gp3[zl]
 
     for half in range(2):
         exchange(*first_peer[half], g2.at[half], g3.at[half], 12 + half, False)
@@ -539,19 +537,8 @@
 
 
 def hand_over(*refs):
-    sems = refs[10]
-    copies = []
     for k in range(5):
-        if k < 2:
-            for l in range(8):
-                copies.append((refs[k].at[l], refs[5 + k].at[l]))
-        else:
-            copies.append((refs[k], refs[5 + k]))
-    copies = [pltpu.make_async_copy(src, dst, sems.at[i]) for i, (src, dst) in enumerate(copies)]
-    for copy in copies:
-        copy.start()
-    for copy in copies:
-        copy.wait()
+        refs[5 + k][...] = refs[k][...]
 
 
 def body(
@@ -583,8 +570,9 @@
         + [vmem((256, 3 * D), F32), vmem((8, 32, D), BF), vmem((8, 32, D), BF), dma((9,))]
         + [vmem((6, 4, 64, 256), F32)]
         + [vmem((256, D), BF), vmem((256, D), BF), vmem((256, 3 * D), BF), vmem((256, D), BF), vmem((256, D), BF), vmem((256, 3 * D), BF)]
-        + [vmem((4, 4, 48, D), BF), vmem((4, 4, 48, D), BF), vmem((2, 4, 24, D), F32)]
-        + [vmem((4, 24, D), BF), vmem((4, 24, D), BF), vmem((4, 24, D), F32)]
+        + [vmem((4, 4, 2, 24, D), BF)]
+        + [vmem((4, 4, 24, D), BF)] * 3
+        + [vmem((4, 24, D), BF)] * 2
         + [vmem((8, 24, 128), F32), vmem((8, 24, 128), F32)]
         + [dma((4,)), dma((4,))]
         + [vmem((10, 8, D), F32), vmem((16, 1, D), F32), vmem((16, 1, D), F32), vmem((1, D), F32), vmem((16, 1, D), F32), vmem((1, D), F32), vmem((16, 1, D), F32)]
@@ -612,8 +600,8 @@
         pattern.reshape(1, 256), qkv_weight, out_weight, score_bias,
     )
     block_out, grad_fields, gp, taps, gain = pl.pallas_call(
-        hand_over, out_shape=results, in_specs=[hbm] * 5, out_specs=(hbm,) * 5,
-        scratch_shapes=[dma((19,))], name="results",
+        hand_over, out_shape=results, in_specs=[vm] * 5, out_specs=(vm,) * 5,
+        name="results",
     )(*out)
     return (block_out, grad_fields, jnp.transpose(gp), taps, gain)
 

time: 124 us -> 96.8 us (0.78)
  Pallas kernels: 123 us -> 96 us
    pallas_call x1, Pallas kernels: 26.7 us -> 2.06 us  [body(): pl.pallas_call(hand_over, out_shape=results, in_specs=[vm] * 5, out_specs...]
    pallas_call x1, Pallas kernels: 96.1 us -> 94 us  [body(): pl.pallas_call(kernel, out_shape=results, in_specs=[hbm] * 8, out_specs=(...]
where the time goes in v6:
time: 96.8 us; the launch traced here: 96.7 us
  Pallas kernels  96 us (99%)
    pallas_call x1, Pallas kernels, body(): pl.pallas_call(kernel, out_shape=results, in_specs=[hbm] * 8, out_specs=(...  94 us
    pallas_call x1, Pallas kernels, body(): pl.pallas_call(hand_over, out_shape=results, in_specs=[vm] * 5, out_specs...  2.06 us

profile of v6, /device:TPU:1, one launch (start us, length us, event | category | flops | bytes accessed | tf_op | source)
XLA Modules:
  0.0 96.7 jit_solution(1999346720553190678)
XLA Ops:
  0.6 94.0 %section.1 = (bf16[8,32,768]{2,1,0:T(8,128)(2,1)}, bf16[8,32,768]{2,1,0:T(8,128)(2,1)}, f32[24,96]{1,0:T(8,128)}, f32[3,3,768]{2,1,0:T(4,128)}, f32[768]{0:T(1024)}) custom-call(bf16[8,32,768]{2,1,0:T(8,128)(2,1)} %fields_hbm.1, bf16[8,32,768]{2,1,0:T(8,128)(2,1)} %cot_hbm.1, f32[3,3,768]{2,1,0:T(4,128)} %taps_hbm.1, f32[768]{0:T(1024)} %gain_hbm.1, ...), custom_call_target="tpu_custom_call" | custom-call | tf_op jit(solution)/shard_map/section/pallas_call | solution.py:588
  94.6 2.1 %results.1 = (bf16[8,32,768]{2,1,0:T(8,128)(2,1)}, bf16[8,32,768]{2,1,0:T(8,128)(2,1)}, f32[24,96]{1,0:T(8,128)}, f32[3,3,768]{2,1,0:T(4,128)}, f32[768]{0:T(1024)}) custom-call(bf16[8,32,768]{2,1,0:T(8,128)(2,1)} %get-tuple-element.15.refs_0_, bf16[8,32,768]{2,1,0:T(8,128)(2,1)} %get-tuple-element.16.refs_1_, f32[24,96]{1,0:T(8,128)} %get-tuple-element.17.refs_2_, ...), custom_call_target="tpu_custom_call" | custom-call | tf_op jit(solution)/shard_map/results/pallas_call | solution.py:602

commit v7 on v6

--- a/solution.py
+++ b/solution.py
@@ -96,7 +96,8 @@
         )
     ):
         loads[name] = pltpu.make_async_copy(src, dst, w_sem.at[i])
-        loads[name].start()
+        if i < 3:
+            loads[name].start()
 
     bar = pltpu.get_barrier_semaphore()
 
@@ -149,8 +150,9 @@
                 device_id=neighbour(*offsets[m]), device_id_type=MESH,
             ).start()
 
-    def halo_wait(rows, cols, corner_to, ss, rs):
-        for kind, ref in enumerate((rows, cols, corner_to)):
+    def halo_wait(kinds, rows, cols, corner_to, ss, rs):
+        for kind in kinds:
+            ref = (rows, cols, corner_to)[kind]
             arrived(ref, ss.at[kind])
             arrived(ref, rs.at[kind])
 
@@ -164,7 +166,7 @@
             shifted[1, r] = f
             shifted[2, r] = pltpu.roll(f, 31, 0)
 
-    def fill_rim(rows, cols, corner):
+    def fill_rows(rows, corner):
         for r, n, mask in ((0, 0, top_mask), (9, 1, bottom_mask)):
             f = rows[n].astype(F32) * mask
             le = corner[2 * n].astype(F32) * mask
@@ -172,6 +174,8 @@
             shifted[0, r] = jnp.where(row32 == 0, le, pltpu.roll(f, 1, 0))
             shifted[1, r] = f
             shifted[2, r] = jnp.where(row32 == 31, ri, pltpu.roll(f, 31, 0))
+
+    def fill_cols(cols):
         le = cols[0].astype(F32)
         ri = cols[1].astype(F32)
         for r in range(1, 9):
@@ -218,6 +222,9 @@
     fill_edges(fields, edges, corners)
     pl.semaphore_wait(bar, 41)
     halo_start((0, 1, 2), fields, edges, corners, rows_in, cols_in, corner_in, halo_s, halo_r)
+
+    for name in ("bias", "taps", "gain", "wqkv", "wo"):
+        loads[name].start()
 
     loads["pat"].wait()
     pat_hot = one_hot(iota2(0) == pat[...])
@@ -241,12 +248,13 @@
         bias_t[q] = jnp.transpose(bias[4 * q : 4 * q + 4].reshape(256, 64))
 
     fill_inside(fields)
-    halo_wait(rows_in, cols_in, corner_in, halo_s, halo_r)
-    exchange(*first_peer[1], c0.at[1], c1.at[1], 5, True)
-    fill_rim(rows_in, cols_in, corner_in)
     loads["taps"].wait()
     loads["gain"].wait()
     gain_row = gain[...].reshape(1, D)
+    halo_f = (rows_in, cols_in, corner_in, halo_s, halo_r)
+    halo_wait((1,), *halo_f)
+    exchange(*first_peer[1], c0.at[1], c1.at[1], 5, True)
+    fill_cols(cols_in)
 
     def conv_row(l, flip):
         out = shifted[1, l + 1]
@@ -270,18 +278,21 @@
         normed_w[l] = (xh * gain_row).astype(BF)
         return carry
 
-    lax.fori_loop(0, 8, norm_row, 0, unroll=2)
+    lax.fori_loop(1, 7, norm_row, 0, unroll=2)
+    halo_wait((0, 2), *halo_f)
+    fill_rows(rows_in, corner_in)
+    norm_row(0, 0)
+    norm_row(7, 0)
     for h in range(2):
         permute_out(perm_out, normed_w, n0, h)
         exchange(*first_peer[h], n0.at[h], n1.at[h], h, True)
-    for h in range(2):
-        exchange(*first_peer[h], c0.at[h], c1.at[h], 4 + h, False)
-        permute_mid(c1, c2, h)
     for h in range(2):
         exchange(*first_peer[h], n0.at[h], n1.at[h], h, False)
         permute_mid(n1, n2, h)
         exchange(*second_peer[h], n2.at[h], n3.at[h], 2 + h, True)
     for h in range(2):
+        exchange(*first_peer[h], c0.at[h], c1.at[h], 4 + h, False)
+        permute_mid(c1, c2, h)
         exchange(*second_peer[h], c2.at[h], c3.at[h], 6 + h, True)
 
     exchange(*second_peer[1], n2.at[1], n3.at[1], 3, False)
@@ -338,7 +349,7 @@
             gqkv[rows, columns(q, 2)] = nn(p.astype(BF), g_bd).astype(BF)
         return carry
 
-    lax.fori_loop(0, 6, attend, 0)
+    lax.fori_loop(0, 6, attend, 0, unroll=2)
 
     loads["wo"].wait()
     for n in range(3):
@@ -393,7 +404,7 @@
         cols = slice(n * 256, (n + 1) * 256)
         grad_att[:, cols] = nt(cot_g[...], wo[cols, :]).astype(BF)
 
-    lax.fori_loop(0, 3, attend_back, 0)
+    lax.fori_loop(0, 3, attend_back, 0, unroll=3)
     core.wait()
     for k in range(4):
         gpa[k] = (gp0[k, :, c].astype(F32) + gpx[k].astype(F32)).astype(BF)
@@ -401,7 +412,7 @@
         gp_y(d)
     for k in range(4):
         gp1[y, k] = gpa[k, y]
-    lax.fori_loop(3, 6, attend_back, 0)
+    lax.fori_loop(3, 6, attend_back, 0, unroll=3)
 
     for half in range(2):
         cols = slice(half * 384, (half + 1) * 384)
@@ -409,14 +420,14 @@
         permute_out(perm_arr, work, g0, half)
         exchange(*second_peer[half], g0.at[half], g1.at[half], 10 + half, True)
 
+    for half in (1, 0):
+        exchange(*second_peer[half], g0.at[half], g1.at[half], 10 + half, False)
+        permute_mid(g1, g2, half)
+        exchange(*first_peer[half], g2.at[half], g3.at[half], 12 + half, True)
+
     exchange(peer_a, me_a, m0, m1, 8, False)
     permute(perm_swap, m1, m2)
     exchange(peer_b, me_b, m2, m3, 9, True)
-
-    for half in range(2):
-        exchange(*second_peer[half], g0.at[half], g1.at[half], 10 + half, False)
-        permute_mid(g1, g2, half)
-        exchange(*first_peer[half], g2.at[half], g3.at[half], 12 + half, True)
 
     gp_arrived(gp1, 3, 0)
     for k in range(4):
@@ -427,13 +438,6 @@
     for d in range(1, 4):
         gp_z(d)
     gp4[zl] = gp3[zl]
-
-    exchange(peer_b, me_b, m2, m3, 9, False)
-    permute(perm_home.at[0], m3, work2)
-    for l in range(8):
-        block_v[l] = (hid[l].astype(F32) + work2[l * 32 : (l + 1) * 32, :].astype(F32)).astype(BF)
-    block_copy = pltpu.make_async_copy(block_v, block_out, out_sem.at[8])
-    block_copy.start()
 
     for half in range(2):
         exchange(*first_peer[half], g2.at[half], g3.at[half], 12 + half, False)
@@ -450,7 +454,12 @@
         mu = jnp.mean(u, axis=-1, keepdims=True)
         mux = jnp.mean(prod * gain_row, axis=-1, keepdims=True)
         gh = cot[l].astype(F32) + rstd[l] * (u - mu - xh * mux)
-        normed_w[l] = gh.astype(BF)
+        ghb = gh.astype(BF)
+        normed_w[l] = ghb
+        ghf = ghb.astype(F32)
+        for i in range(3):
+            for j in range(3):
+                acc[3 * i + j] += jnp.sum((shifted[j, l + i] * ghf).reshape(4, 8, D), axis=0)
         return carry
 
     halo_g = (normed_w, edges_g, corners_g, rows_in_g, cols_in_g, corner_in_g, halo_gs, halo_gr)
@@ -461,14 +470,6 @@
     fill_edges(normed_w, edges_g, corners_g)
     halo_start((1, 2), *halo_g)
 
-    def tap_sums(l, carry):
-        gh = normed_w[l].astype(F32)
-        for i in range(3):
-            for j in range(3):
-                acc[3 * i + j] += jnp.sum((shifted[j, l + i] * gh).reshape(4, 8, D), axis=0)
-        return carry
-
-    lax.fori_loop(0, 8, tap_sums, 0, unroll=2)
     for k in range(16):
         if k < 10:
             s0[k] = jnp.sum(acc[k], axis=0, keepdims=True)
@@ -495,10 +496,26 @@
 
     sums(peer_b, me_b, s0, s1, 0, False, True)
     fill_inside(normed_w)
+    exchange(peer_b, me_b, m2, m3, 9, False)
+    permute(perm_home.at[0], m3, work2)
+    for l in range(8):
+        block_v[l] = (hid[l].astype(F32) + work2[l * 32 : (l + 1) * 32, :].astype(F32)).astype(BF)
+    block_copy = pltpu.make_async_copy(block_v, block_out, out_sem.at[8])
+    block_copy.start()
 
     sums(peer_b, me_b, s0, s1, 0, False, False)
     s2[...] = jnp.sum(s1[...], axis=0)
     sums(peer_a, me_a, s2, s3, 1, True, True)
+
+    def grad_row(l, carry):
+        grad_v[l] = conv_row(l, True).astype(BF)
+        pltpu.make_async_copy(grad_v.at[l], grad_fields.at[l], out_sem.at[l]).start()
+        return carry
+
+    halo_b = (rows_in_g, cols_in_g, corner_in_g, halo_gs, halo_gr)
+    halo_wait((1,), *halo_b)
+    fill_cols(cols_in_g)
+    lax.fori_loop(1, 7, grad_row, 0, unroll=2)
 
     gp_arrived(gp4, 3, 2)
     total = gp4[0].astype(F32)
@@ -515,15 +532,10 @@
     s4[...] = jnp.sum(s3[...], axis=0) * TOTAL_SCALE
     sums(peer_b, me_b, s4, s5, 2, True, True)
 
-    halo_wait(rows_in_g, cols_in_g, corner_in_g, halo_gs, halo_gr)
-    fill_rim(rows_in_g, cols_in_g, corner_in_g)
-
-    def grad_row(l, carry):
-        grad_v[l] = conv_row(l, True).astype(BF)
-        pltpu.make_async_copy(grad_v.at[l], grad_fields.at[l], out_sem.at[l]).start()
-        return carry
-
-    lax.fori_loop(0, 8, grad_row, 0, unroll=2)
+    halo_wait((0, 2), *halo_b)
+    fill_rows(rows_in_g, corner_in_g)
+    grad_row(0, 0)
+    grad_row(7, 0)
 
     gp_arrived(gp7, 7, 3)
     gp_out[...] = (jnp.sum(gp7[...], axis=0) * TOTAL_SCALE)[:, 0:96]

time: 96.8 us -> 86.1 us (0.89)
  Pallas kernels: 96 us -> 85.3 us
    pallas_call x1, Pallas kernels: 94 us -> 83.3 us  [body(): pl.pallas_call(kernel, out_shape=results, in_specs=[hbm] * 8, out_specs=(...]
where the time goes in v7:
time: 86.1 us; the launch traced here: 86 us
  Pallas kernels  85.3 us (99%)
    pallas_call x1, Pallas kernels, body(): pl.pallas_call(kernel, out_shape=results, in_specs=[hbm] * 8, out_specs=(...  83.3 us
    pallas_call x1, Pallas kernels, body(): pl.pallas_call(hand_over, out_shape=results, in_specs=[vm] * 5, out_specs...  2.06 us

profile of v7, /device:TPU:1, one launch (start us, length us, event | category | flops | bytes accessed | tf_op | source)
XLA Modules:
  0.0 86.0 jit_solution(5115951271746004957)
XLA Ops:
  0.6 83.3 %section.1 = (bf16[8,32,768]{2,1,0:T(8,128)(2,1)}, bf16[8,32,768]{2,1,0:T(8,128)(2,1)}, f32[24,96]{1,0:T(8,128)}, f32[3,3,768]{2,1,0:T(4,128)}, f32[768]{0:T(1024)}) custom-call(bf16[8,32,768]{2,1,0:T(8,128)(2,1)} %fields_hbm.1, bf16[8,32,768]{2,1,0:T(8,128)(2,1)} %cot_hbm.1, f32[3,3,768]{2,1,0:T(4,128)} %taps_hbm.1, f32[768]{0:T(1024)} %gain_hbm.1, ...), custom_call_target="tpu_custom_call" | custom-call | tf_op jit(solution)/shard_map/section/pallas_call | solution.py:600
  83.9 2.1 %results.1 = (bf16[8,32,768]{2,1,0:T(8,128)(2,1)}, bf16[8,32,768]{2,1,0:T(8,128)(2,1)}, f32[24,96]{1,0:T(8,128)}, f32[3,3,768]{2,1,0:T(4,128)}, f32[768]{0:T(1024)}) custom-call(bf16[8,32,768]{2,1,0:T(8,128)(2,1)} %get-tuple-element.15.refs_0_, bf16[8,32,768]{2,1,0:T(8,128)(2,1)} %get-tuple-element.16.refs_1_, f32[24,96]{1,0:T(8,128)} %get-tuple-element.17.refs_2_, ...), custom_call_target="tpu_custom_call" | custom-call | tf_op jit(solution)/shard_map/results/pallas_call | solution.py:614

commit v8 on v7

--- a/solution.py
+++ b/solution.py
@@ -113,7 +113,7 @@
         pl.semaphore_signal(
             bar, inc=1, device_id=device(rem(x + d, 4), y, rem(z + 4, 8), c), device_id_type=MESH
         )
-    lax.fori_loop(1, 16, greet, 0)
+    lax.fori_loop(1, 16, greet, 0, unroll=15)
 
     row8 = lax.broadcasted_iota(jnp.int32, (8, D), 0)
     row32 = lax.broadcasted_iota(jnp.int32, (32, D), 0)
@@ -242,6 +242,7 @@
     permute_out(perm_out, cot, c0, 0)
     exchange(*first_peer[0], c0.at[0], c1.at[0], 4, True)
     permute_out(perm_out, cot, c0, 1)
+    exchange(*first_peer[1], c0.at[1], c1.at[1], 5, True)
 
     loads["bias"].wait()
     for q in range(6):
@@ -253,7 +254,6 @@
     gain_row = gain[...].reshape(1, D)
     halo_f = (rows_in, cols_in, corner_in, halo_s, halo_r)
     halo_wait((1,), *halo_f)
-    exchange(*first_peer[1], c0.at[1], c1.at[1], 5, True)
     fill_cols(cols_in)
 
     def conv_row(l, flip):
@@ -309,11 +309,10 @@
 
     lane_head = lax.broadcasted_iota(jnp.int32, (64, 128), 1) >> 5
 
+    own_head = [one_hot(lane_head == e) for e in range(4)]
+
     def spread(v):
-        vf = v.astype(F32)
-        return jnp.concatenate(
-            [jnp.where(lane_head == e, vf, 0.0).astype(BF) for e in range(4)], axis=0
-        )
+        return jnp.concatenate([v * own_head[e] for e in range(4)], axis=0)
 
     def gather(v):
         out = jnp.zeros((64, 128), F32)

time: 86.1 us -> 85.9 us (level)
  no operation moved by 1% of the time
where the time goes in v8:
time: 85.9 us; the launch traced here: 85.8 us
  Pallas kernels  85.1 us (99%)
    pallas_call x1, Pallas kernels, body(): pl.pallas_call(kernel, out_shape=results, in_specs=[hbm] * 8, out_specs=(...  83.1 us
    pallas_call x1, Pallas kernels, body(): pl.pallas_call(hand_over, out_shape=results, in_specs=[vm] * 5, out_specs...  2.06 us

profile of v8, /device:TPU:1, one launch (start us, length us, event | category | flops | bytes accessed | tf_op | source)
XLA Modules:
  0.0 85.8 jit_solution(17012522680937900808)
XLA Ops:
  0.6 83.1 %section.1 = (bf16[8,32,768]{2,1,0:T(8,128)(2,1)}, bf16[8,32,768]{2,1,0:T(8,128)(2,1)}, f32[24,96]{1,0:T(8,128)}, f32[3,3,768]{2,1,0:T(4,128)}, f32[768]{0:T(1024)}) custom-call(bf16[8,32,768]{2,1,0:T(8,128)(2,1)} %fields_hbm.1, bf16[8,32,768]{2,1,0:T(8,128)(2,1)} %cot_hbm.1, f32[3,3,768]{2,1,0:T(4,128)} %taps_hbm.1, f32[768]{0:T(1024)} %gain_hbm.1, ...), custom_call_target="tpu_custom_call" | custom-call | tf_op jit(solution)/shard_map/section/pallas_call | solution.py:599
  83.7 2.1 %results.1 = (bf16[8,32,768]{2,1,0:T(8,128)(2,1)}, bf16[8,32,768]{2,1,0:T(8,128)(2,1)}, f32[24,96]{1,0:T(8,128)}, f32[3,3,768]{2,1,0:T(4,128)}, f32[768]{0:T(1024)}) custom-call(bf16[8,32,768]{2,1,0:T(8,128)(2,1)} %get-tuple-element.15.refs_0_, bf16[8,32,768]{2,1,0:T(8,128)(2,1)} %get-tuple-element.16.refs_1_, f32[24,96]{1,0:T(8,128)} %get-tuple-element.17.refs_2_, ...), custom_call_target="tpu_custom_call" | custom-call | tf_op jit(solution)/shard_map/results/pallas_call | solution.py:613

commit v9 on v8

--- a/solution.py
+++ b/solution.py
@@ -361,6 +361,43 @@
         exchange(*second_peer[h], c2.at[h], c3.at[h], 6 + h, False)
         permute_in(perm_pos, c3, cot_g, h)
 
+    def gp_y(d):
+        k = rem(y + d, 4)
+        pltpu.make_async_remote_copy(
+            src_ref=gpa.at[:, k], dst_ref=gp1.at[y], send_sem=gp_s.at[0], recv_sem=gp_r.at[0],
+            device_id=device(x, k, z, c), device_id_type=MESH,
+        ).start()
+
+    def gp_z(d):
+        k = rem(zl + d, 4)
+        pltpu.make_async_remote_copy(
+            src_ref=gp3.at[k], dst_ref=gp4.at[zl], send_sem=gp_s.at[2], recv_sem=gp_r.at[2],
+            device_id=device(x, y, zh * 4 + k, c), device_id_type=MESH,
+        ).start()
+
+    def gp_l(d):
+        k = rem(a + d, 8)
+        pltpu.make_async_remote_copy(
+            src_ref=gp6.at[k], dst_ref=gp7.at[a], send_sem=gp_s.at[3], recv_sem=gp_r.at[3],
+            device_id=(k, b), device_id_type=MESH,
+        ).start()
+
+    def gp_arrived(ref, n, stage):
+        arrived(ref.at[pl.ds(0, n)], gp_s.at[stage])
+        arrived(ref.at[pl.ds(0, n)], gp_r.at[stage])
+
+    for n in range(3):
+        cols = slice(n * 256, (n + 1) * 256)
+        grad_att[:, cols] = nt(cot_g[...], wo[cols, :]).astype(BF)
+
+    lax.fori_loop(0, 6, attend_back, 0, unroll=3)
+
+    for half in range(2):
+        cols = slice(half * 384, (half + 1) * 384)
+        work[:, cols] = nt(gqkv[...], wqkv[cols, :]).astype(BF)
+        permute_out(perm_arr, work, g0, half)
+        exchange(*second_peer[half], g0.at[half], g1.at[half], 10 + half, True)
+
     def outer(n, carry):
         cols = pl.ds(pl.multiple_of(n * 384, 128), 384)
         got = tn(cot_g[:, cols], att[...])
@@ -374,36 +411,12 @@
     )
     core.start()
 
-    def gp_y(d):
-        k = rem(y + d, 4)
-        pltpu.make_async_remote_copy(
-            src_ref=gpa.at[:, k], dst_ref=gp1.at[y], send_sem=gp_s.at[0], recv_sem=gp_r.at[0],
-            device_id=device(x, k, z, c), device_id_type=MESH,
-        ).start()
-
-    def gp_z(d):
-        k = rem(zl + d, 4)
-        pltpu.make_async_remote_copy(
-            src_ref=gp3.at[k], dst_ref=gp4.at[zl], send_sem=gp_s.at[2], recv_sem=gp_r.at[2],
-            device_id=device(x, y, zh * 4 + k, c), device_id_type=MESH,
-        ).start()
-
-    def gp_l(d):
-        k = rem(a + d, 8)
-        pltpu.make_async_remote_copy(
-            src_ref=gp6.at[k], dst_ref=gp7.at[a], send_sem=gp_s.at[3], recv_sem=gp_r.at[3],
-            device_id=(k, b), device_id_type=MESH,
-        ).start()
-
-    def gp_arrived(ref, n, stage):
-        arrived(ref.at[pl.ds(0, n)], gp_s.at[stage])
-        arrived(ref.at[pl.ds(0, n)], gp_r.at[stage])
-
-    for n in range(3):
-        cols = slice(n * 256, (n + 1) * 256)
-        grad_att[:, cols] = nt(cot_g[...], wo[cols, :]).astype(BF)
-
-    lax.fori_loop(0, 3, attend_back, 0, unroll=3)
+    def forward_half(half):
+        exchange(*second_peer[half], g0.at[half], g1.at[half], 10 + half, False)
+        permute_mid(g1, g2, half)
+        exchange(*first_peer[half], g2.at[half], g3.at[half], 12 + half, True)
+
+    forward_half(1)
     core.wait()
     for k in range(4):
         gpa[k] = (gp0[k, :, c].astype(F32) + gpx[k].astype(F32)).astype(BF)
@@ -411,18 +424,7 @@
         gp_y(d)
     for k in range(4):
         gp1[y, k] = gpa[k, y]
-    lax.fori_loop(3, 6, attend_back, 0, unroll=3)
-
-    for half in range(2):
-        cols = slice(half * 384, (half + 1) * 384)
-        work[:, cols] = nt(gqkv[...], wqkv[cols, :]).astype(BF)
-        permute_out(perm_arr, work, g0, half)
-        exchange(*second_peer[half], g0.at[half], g1.at[half], 10 + half, True)
-
-    for half in (1, 0):
-        exchange(*second_peer[half], g0.at[half], g1.at[half], 10 + half, False)
-        permute_mid(g1, g2, half)
-        exchange(*first_peer[half], g2.at[half], g3.at[half], 12 + half, True)
+    forward_half(0)
 
     exchange(peer_a, me_a, m0, m1, 8, False)
     permute(perm_swap, m1, m2)

time: 85.9 us -> 90.7 us (1.056)
  Pallas kernels: 85.1 us -> 90 us
    pallas_call x1, Pallas kernels: 83.1 us -> 87.9 us  [body(): pl.pallas_call(kernel, out_shape=results, in_specs=[hbm] * 8, out_specs=(...]
where the time goes in v9:
time: 90.7 us; the launch traced here: 90.6 us
  Pallas kernels  90 us (99%)
    pallas_call x1, Pallas kernels, body(): pl.pallas_call(kernel, out_shape=results, in_specs=[hbm] * 8, out_specs=(...  87.9 us
    pallas_call x1, Pallas kernels, body(): pl.pallas_call(hand_over, out_shape=results, in_specs=[vm] * 5, out_specs...  2.06 us

profile of v9, /device:TPU:1, one launch (start us, length us, event | category | flops | bytes accessed | tf_op | source)
XLA Modules:
  0.0 90.6 jit_solution(8230842676307497187)
XLA Ops:
  0.6 87.9 %section.1 = (bf16[8,32,768]{2,1,0:T(8,128)(2,1)}, bf16[8,32,768]{2,1,0:T(8,128)(2,1)}, f32[24,96]{1,0:T(8,128)}, f32[3,3,768]{2,1,0:T(4,128)}, f32[768]{0:T(1024)}) custom-call(bf16[8,32,768]{2,1,0:T(8,128)(2,1)} %fields_hbm.1, bf16[8,32,768]{2,1,0:T(8,128)(2,1)} %cot_hbm.1, f32[3,3,768]{2,1,0:T(4,128)} %taps_hbm.1, f32[768]{0:T(1024)} %gain_hbm.1, ...), custom_call_target="tpu_custom_call" | custom-call | tf_op jit(solution)/shard_map/section/pallas_call | solution.py:601
  88.5 2.1 %results.1 = (bf16[8,32,768]{2,1,0:T(8,128)(2,1)}, bf16[8,32,768]{2,1,0:T(8,128)(2,1)}, f32[24,96]{1,0:T(8,128)}, f32[3,3,768]{2,1,0:T(4,128)}, f32[768]{0:T(1024)}) custom-call(bf16[8,32,768]{2,1,0:T(8,128)(2,1)} %get-tuple-element.15.refs_0_, bf16[8,32,768]{2,1,0:T(8,128)(2,1)} %get-tuple-element.16.refs_1_, f32[24,96]{1,0:T(8,128)} %get-tuple-element.17.refs_2_, ...), custom_call_target="tpu_custom_call" | custom-call | tf_op jit(solution)/shard_map/results/pallas_call | solution.py:615

commit v10 on v8

--- a/solution.py
+++ b/solution.py
@@ -548,8 +548,25 @@
 
 
 def hand_over(*refs):
+    held, sem_in, sem_out = refs[10:15], refs[15], refs[16]
+    moves = []
     for k in range(5):
-        refs[5 + k][...] = refs[k][...]
+        parts = [slice(0, 4), slice(4, 8)] if k < 2 else [slice(None)]
+        for part in parts:
+            i = len(moves)
+            moves.append(
+                (
+                    pltpu.make_async_copy(refs[k].at[part], held[k].at[part], sem_in.at[i]),
+                    pltpu.make_async_copy(held[k].at[part], refs[5 + k].at[part], sem_out.at[i]),
+                )
+            )
+    for load, store in moves:
+        load.start()
+    for load, store in moves:
+        load.wait()
+        store.start()
+    for load, store in moves:
+        store.wait()
 
 
 def body(
@@ -611,7 +628,8 @@
         pattern.reshape(1, 256), qkv_weight, out_weight, score_bias,
     )
     block_out, grad_fields, gp, taps, gain = pl.pallas_call(
-        hand_over, out_shape=results, in_specs=[vm] * 5, out_specs=(vm,) * 5,
+        hand_over, out_shape=results, in_specs=[hbm] * 5, out_specs=(hbm,) * 5,
+        scratch_shapes=[vmem(r.shape, r.dtype) for r in results] + [dma((7,)), dma((7,))],
         name="results",
     )(*out)
     return (block_out, grad_fields, jnp.transpose(gp), taps, gain)

time: 85.9 us -> 85.9 us (level)
  no operation moved by 1% of the time
where the time goes in v10:
time: 85.9 us; the launch traced here: 85.8 us
  Pallas kernels  85.1 us (99%)
    pallas_call x1, Pallas kernels, body(): pl.pallas_call(kernel, out_shape=results, in_specs=[hbm] * 8, out_specs=(...  83.1 us
    pallas_call x1, Pallas kernels, body(): pl.pallas_call(hand_over, out_shape=results, in_specs=[hbm] * 5, out_spec...  2.03 us

profile of v10, /device:TPU:1, one launch (start us, length us, event | category | flops | bytes accessed | tf_op | source)
XLA Modules:
  0.0 85.8 jit_solution(7598504867057586354)
XLA Ops:
  0.6 83.1 %section.1 = (bf16[8,32,768]{2,1,0:T(8,128)(2,1)}, bf16[8,32,768]{2,1,0:T(8,128)(2,1)}, f32[24,96]{1,0:T(8,128)}, f32[3,3,768]{2,1,0:T(4,128)}, f32[768]{0:T(1024)}) custom-call(bf16[8,32,768]{2,1,0:T(8,128)(2,1)} %fields_hbm.1, bf16[8,32,768]{2,1,0:T(8,128)(2,1)} %cot_hbm.1, f32[3,3,768]{2,1,0:T(4,128)} %taps_hbm.1, f32[768]{0:T(1024)} %gain_hbm.1, ...), custom_call_target="tpu_custom_call" | custom-call | tf_op jit(solution)/shard_map/section/pallas_call | solution.py:616
  83.7 2.0 %results.1 = (bf16[8,32,768]{2,1,0:T(8,128)(2,1)}, bf16[8,32,768]{2,1,0:T(8,128)(2,1)}, f32[24,96]{1,0:T(8,128)}, f32[3,3,768]{2,1,0:T(4,128)}, f32[768]{0:T(1024)}) custom-call(bf16[8,32,768]{2,1,0:T(8,128)(2,1)} %get-tuple-element.15.refs_0_, bf16[8,32,768]{2,1,0:T(8,128)(2,1)} %get-tuple-element.16.refs_1_, f32[24,96]{1,0:T(8,128)} %get-tuple-element.17.refs_2_, ...), custom_call_target="tpu_custom_call" | custom-call | tf_op jit(solution)/shard_map/results/pallas_call | solution.py:630
